TPU v7x, 32 devices: a whole 2x2x4 slice. The times are simulated.
32 devices in a mesh: blk: 8 (over z, x), map: 4 (over y, core).
Axes of the slice: x: 2, y: 2, z: 4, core: 2. Of those that a mesh axis runs over, the one named last changes fastest.
Arguments:
- sky_maps: bfloat16 [32, 10, 32768], P(('blk', 'map')), may hold values from -6 to 6
- cycle_number: int32 [32], replicated, may hold values from 8192 to 24576
- legendre_starts: float32 [2, 512, 64, 32], P(None, 'blk', 'map'), may hold values from -6 to 6
Outputs:
- harmonics: bfloat16 [512, 20, 8192], P('blk', None, 'map')
- spectra: float32 [4, 10, 10, 2048], P('map', None, None, 'blk')
All inputs are finite; a program needn't handle non-finite values.
Results may differ from a plain program's by a relative error of at most 0.0071.
Values may be sent and summed in bfloat16 or wider, within the bound.
A program may use at most 128 MiB of HBM per device.

v0:
```python
import math

import jax
import jax.numpy as jnp
from jax import lax
from jax.sharding import PartitionSpec as P

NSIDE = 8192
RES = 128
MGRP = 4
MSTART = 4096
LSTART = 8192
LBLK = 128


def shortened(array):

    def short(part):
        return part.astype(jnp.bfloat16) if part.dtype == jnp.float32 else part

    return jax.tree.map(short, array)


def cycle_height(cycle_ids):
    return (4.0 * NSIDE - 2.0 * cycle_ids.astype(jnp.float32)) / (3.0 * NSIDE)


def dft_tables(cycle_len):
    low_len = cycle_len // RES
    residue = jnp.arange(RES, dtype=jnp.int32)
    turn_one = residue[:, None] * residue[None, :] % RES
    angle_one = 2.0 * math.pi / RES * turn_one.astype(jnp.float32)
    first_table = jnp.concatenate([jnp.cos(angle_one), -jnp.sin(angle_one)], axis=1).astype(
        jnp.bfloat16
    )
    column_group = jnp.arange(MGRP, dtype=jnp.int32)
    sample = jnp.arange(low_len, dtype=jnp.int32)
    m_value = MSTART + RES * column_group[:, None, None] + residue[None, None, :]
    turn_two = m_value * sample[None, :, None] % cycle_len
    angle_two = 2.0 * math.pi / cycle_len * turn_two.astype(jnp.float32)
    twiddle_re = jnp.cos(angle_two).astype(jnp.bfloat16)
    twiddle_im = (-jnp.sin(angle_two)).astype(jnp.bfloat16)
    return (first_table, twiddle_re, twiddle_im)


def cycle_transform(cycle_rows, parity, tables):
    first_table, twiddle_re, twiddle_im = tables
    cycle_count, maps_count, cycle_len = cycle_rows.shape
    low_len = cycle_len // RES
    folded = cycle_rows.reshape(cycle_count, maps_count, RES, low_len)
    section_one = jnp.einsum(
        "rnaj,ak->rnjk", folded, first_table, preferred_element_type=jnp.float32
    )
    section_one = section_one.astype(jnp.bfloat16)
    part_re = section_one[..., :RES]
    part_im = section_one[..., RES:]
    real_sum = jnp.einsum(
        "rnjk,cjk->rnck", part_re, twiddle_re, preferred_element_type=jnp.float32
    ) - jnp.einsum("rnjk,cjk->rnck", part_im, twiddle_im, preferred_element_type=jnp.float32)
    imag_sum = jnp.einsum(
        "rnjk,cjk->rnck", part_im, twiddle_re, preferred_element_type=jnp.float32
    ) + jnp.einsum("rnjk,cjk->rnck", part_re, twiddle_im, preferred_element_type=jnp.float32)
    column_group = jnp.arange(MGRP, dtype=jnp.int32)
    residue = jnp.arange(RES, dtype=jnp.int32)
    m_value = MSTART + RES * column_group[:, None] + residue[None, :]
    shifted = m_value[None, :, :] * parity[:, None, None] % (2 * cycle_len)
    phase_angle = math.pi / cycle_len * shifted.astype(jnp.float32)
    cos_part = jnp.cos(phase_angle)[:, None]
    sin_part = jnp.sin(phase_angle)[:, None]
    factor = 1.0 / math.sqrt(cycle_len)
    out_re = factor * (cos_part * real_sum + sin_part * imag_sum)
    out_im = factor * (cos_part * imag_sum - sin_part * real_sum)
    return jnp.stack([out_re, out_im], axis=1).astype(jnp.bfloat16)


def legendre_rows(start_pair, height, m_float, first_l):
    m_column = m_float[:, None]

    def recur_coef(degree):
        return jnp.sqrt((4.0 * degree * degree - 1.0) / ((degree - m_column) * (degree + m_column)))

    base_l = first_l.astype(jnp.float32)
    value_older = start_pair[0]
    value_newer = start_pair[1]
    prior_coef = recur_coef(base_l - 1.0)
    height_row = height[None, :]
    stacked_rows = []
    for offset in range(LBLK):
        present_coef = recur_coef(base_l + offset)
        value_now = present_coef * (height_row * value_newer - value_older / prior_coef)
        stacked_rows.append(value_now)
        value_older = value_newer
        value_newer = value_now
        prior_coef = present_coef
    return jnp.stack(stacked_rows, axis=1)


def body(sky_maps, cycle_number, legendre_starts):
    own_cycles, maps_count, cycle_len = sky_maps.shape
    tables = dft_tables(cycle_len)
    map_total = lax.axis_size("map")
    blk_total = lax.axis_size("blk")
    first_row = (lax.axis_index("blk") * map_total + lax.axis_index("map")) * own_cycles
    own_numbers = lax.dynamic_slice_in_dim(cycle_number, first_row, own_cycles)
    parity = (own_numbers - NSIDE + 1) % 2
    local_modes = cycle_transform(sky_maps, parity, tables)
    grouped = lax.all_gather(local_modes, "map", axis=0, tiled=True)
    regrouped = lax.all_to_all(grouped, "blk", split_axis=4, concat_axis=0, tiled=True)
    ordered = jnp.transpose(regrouped, (4, 3, 1, 2, 0))
    local_cols = ordered.shape[0] * ordered.shape[1]
    cycle_modes = ordered.reshape(local_cols, 2 * maps_count, -1)
    heights = cycle_height(cycle_number)
    column = lax.axis_index("blk") * local_cols + jnp.arange(local_cols, dtype=jnp.int32)
    m_float = (MSTART + RES * (column % MGRP) + column // MGRP).astype(jnp.float32)
    block_count = legendre_starts.shape[2]
    local_len = block_count * LBLK
    first_l = LSTART + lax.axis_index("map") * local_len
    cycle_scale = 1.0 / math.sqrt(cycle_modes.shape[-1])

    def one_block(block_index):
        start_pair = lax.dynamic_index_in_dim(legendre_starts, block_index, 2, keepdims=False)
        legendre_tile = legendre_rows(
            start_pair, heights, m_float, first_l + block_index * LBLK
        ).astype(jnp.bfloat16)
        projected = (
            jnp.einsum(
                "qlr,qnr->qnl", legendre_tile, cycle_modes, preferred_element_type=jnp.float32
            )
            * cycle_scale
        )
        return projected.astype(jnp.bfloat16)

    blocks_out = lax.map(one_block, jnp.arange(block_count, dtype=jnp.int32))
    harmonics = jnp.transpose(blocks_out, (1, 2, 0, 3)).reshape(
        local_cols, 2 * maps_count, local_len
    )
    total_cols = MGRP * RES
    spread = harmonics.reshape(local_cols, 2 * maps_count, blk_total, local_len // blk_total)
    spread = jnp.transpose(spread, (2, 3, 1, 0))
    received = lax.all_to_all(
        shortened(spread), "blk", split_axis=0, concat_axis=3, tiled=True
    ).astype(spread.dtype)
    item_count = received.shape[1]
    split_piece = received.reshape(item_count, 2, maps_count, received.shape[3])
    cross_sum = jnp.einsum(
        "gciq,gcjq->ijg", split_piece, split_piece, preferred_element_type=jnp.float32
    )
    owned = (cross_sum / total_cols)[None]
    return (harmonics, owned)


def solution(mesh):
    return jax.shard_map(
        body,
        mesh=mesh,
        in_specs=(P(("blk", "map"), None, None), P(), P(None, "blk", "map", None)),
        out_specs=(P("blk", None, "map"), P("map", None, None, "blk")),
        check_vma=False,
    )
```

profile of v0, /device:TPU:0, one launch (start us, length us, event | category | flops | bytes accessed | tf_op | source)
XLA Modules:
  0.0 573.5 jit_solution(4679751981461542996)
XLA Ops:
  0.6 1.2 dynamic_slice.19
  3.4 1.5 copy.5445
  5.4 5.2 fusion.403
  10.6 5.2 fusion.407
  15.8 5.3 fusion.401
  21.0 5.3 fusion.413
  26.6 6.3 %all_gather.3 = bf16[4,2,10,4,128]{4,3,2,1,0:T(4,128)(2,1)S(1)} all-gather(bf16[1,2,10,4,128]{4,3,2,1,0:T(4,128)(2,1)S(1)} %pad_maximum_fusion), channel_id=1, replica_groups=mesh['blk'=8,'map'=4] {'map'}, dimensions={0}, use_global_device_ids=true | all-gather | bytes 102400 | tf_op jit(solution)/shard_map/all_gather | solution.py:107
  32.9 1.0 copy.5369
  33.9 2.5 reshape.54429
  36.4 6.8 %all-to-all-start = ((bf16[8,2,2560]{2,1,0:T(2,128)(2,1)}), bf16[8,2,2560]{2,1,0:T(2,128)(2,1)S(1)}, u32[]{:S(2)}, u32[]{:S(2)}) async-start(bf16[8,2,2560]{2,1,0:T(2,128)(2,1)} %reshape.54429), calls=%async_computation | async-start | bytes 163840 | tf_op jit(solution)/shard_map/all_to_all | solution.py:108
  43.2 6.9 %all-to-all-done = bf16[8,2,2560]{2,1,0:T(2,128)(2,1)S(1)} async-done(((bf16[8,2,2560]{2,1,0:T(2,128)(2,1)}), bf16[8,2,2560]{2,1,0:T(2,128)(2,1)S(1)}, u32[]{:S(2)}, u32[]{:S(2)}) %all-to-all-start) | async-done | bytes 81952 | tf_op jit(solution)/shard_map/all_to_all | solution.py:108
  50.1 2.5 reshape.54430
  52.6 3.0 copy.5371
  56.2 338.8 %while.14 = (s32[]{:T(128)}, bf16[16,64,20,128]{3,2,1,0:T(8,128)(2,1)}, s32[16]{0:T(128)S(1)}, s32[]{:T(128)}, f32[32]{0:T(128)S(1)}, /*index=5*/f32[2,64,16,32]...) while((s32[]{:T(128)}, ...), condition=%wide.region_1.2_spmd.clone, body=%wide.region_0.1_spmd.clone.sunk | while | flops 13797643 | bytes 9676187 | solution.py:133
  62.1 0.7 constant_dynamic-slice_fusion.3
  74.7 1.6 copy.5465
  76.3 1.1 fusion.586
  83.3 0.7 constant_dynamic-slice_fusion.3
  95.9 1.6 copy.5465
  97.4 1.1 fusion.586
  104.4 0.7 constant_dynamic-slice_fusion.3
  117.0 1.6 copy.5465
  118.6 1.1 fusion.586
  138.2 1.6 copy.5465
  139.7 1.1 fusion.586
  159.3 1.6 copy.5465
  160.9 1.1 fusion.586
  167.9 0.7 constant_dynamic-slice_fusion.3
  180.4 1.6 copy.5465
  182.0 1.1 fusion.586
  189.0 0.7 constant_dynamic-slice_fusion.3
  201.6 1.6 copy.5465
  203.2 1.1 fusion.586
  210.2 0.7 constant_dynamic-slice_fusion.3
  222.8 1.6 copy.5465
  224.4 1.1 fusion.586
  231.4 0.7 constant_dynamic-slice_fusion.3
  244.0 1.6 copy.5465
  245.5 1.1 fusion.586
  265.1 1.6 copy.5465
  266.7 1.1 fusion.586
  286.3 1.6 copy.5465
  287.9 1.1 fusion.586
  307.4 1.6 copy.5465
  309.0 1.1 fusion.586
  328.6 1.6 copy.5465
  330.2 1.1 fusion.586
  349.8 1.6 copy.5465
  351.3 1.1 fusion.586
  370.9 1.6 copy.5465
  372.5 1.1 fusion.586
  392.1 1.6 copy.5465
  393.7 1.1 fusion.586
  395.0 11.2 %copy.5376 = bf16[64,20,16,128]{3,2,1,0:T(8,128)(2,1)} copy(bf16[64,20,16,128]{3,1,0,2:T(8,128)(2,1)} %bitcast.458) | data formatting | bytes 10485760 | tf_op jit(solution)/shard_map/transpose | solution.py:134
  406.2 8.5 %reshape_reshape.3 = bf16[64,20,8,256]{3,2,1,0:T(8,128)(2,1)} reshape(bf16[64,20,16,128]{3,2,1,0:T(8,128)(2,1)} %copy.5376) | data formatting | bytes 10485760 | tf_op jit(solution)/shard_map/reshape;reshape | solution.py:138
  414.7 7.7 %copy.5377 = bf16[8,256,20,64]{1,3,2,0:T(8,128)(2,1)} copy(bf16[8,256,20,64]{1,0,2,3:T(8,128)(2,1)} %bitcast.460) | data formatting | bytes 10485760 | tf_op jit(solution)/shard_map/transpose | solution.py:139
  422.4 4.9 all-to-all-start.1
  427.4 8.5 %copy.5375 = bf16[64,20,16,128]{3,2,0,1:T(8,128)(2,1)} copy(bf16[64,20,16,128]{3,1,0,2:T(8,128)(2,1)} %bitcast.459) | data formatting | bytes 10485760 | tf_op jit(solution)/shard_map/transpose | solution.py:134
  435.9 8.8 %reshape.54425 = bf16[64,20,2048]{2,0,1:T(8,128)(2,1)} reshape(bf16[64,20,16,128]{3,2,0,1:T(8,128)(2,1)} %copy.5375) | data formatting | bytes 10485760 | tf_op jit(solution)/shard_map/reshape | solution.py:134
  444.6 97.8 %all-to-all-done.1 = bf16[8,256,20,64]{1,3,2,0:T(8,128)(2,1)} async-done(((bf16[8,256,20,64]{1,3,2,0:T(8,128)(2,1)}), bf16[8,256,20,64]{1,3,2,0:T(8,128)(2,1)}, u32[]{:S(2)}, u32[]{:S(2)}) %all-to-all-start.1) | async-done | bytes 5242912 | tf_op jit(solution)/shard_map/all_to_all | solution.py:140
  542.4 5.6 copy.5379
  548.0 14.1 %copy.5380 = bf16[256,2,10,512]{3,2,1,0:T(8,128)(2,1)} copy(bf16[256,2,10,512]{0,3,2,1:T(8,128)(2,1)} %bitcast.461) | data formatting | bytes 10485760 | tf_op jit(solution)/shard_map/reshape | solution.py:144
  562.1 9.7 %fusion.399 = f32[1,10,10,256]{1,2,3,0:T(8,128)S(1)} fusion(bf16[256,2,10,512]{3,2,1,0:T(8,128)(2,1)} %copy.5380), kind=kOutput, calls=%fused_computation.965 | convolution fusion | flops 52454400 | bytes 5345280 | tf_op jit(solution)/shard_map/gciq,gcjq->ijg/dot_general | solution.py:145
  571.8 1.4 copy.5382
  (3196 shorter events, 233.7 us)
Async XLA Ops:
  21.0 22.1 %copy-start = (s32[32]{0:T(128)S(1)}, s32[32]{0:T(128)}, u32[]{:S(2)}) copy-start(s32[32]{0:T(128)} %param.6) | copy-start | bytes 388
  36.4 13.8 %all-to-all-start = ((bf16[8,2,2560]{2,1,0:T(2,128)(2,1)}), bf16[8,2,2560]{2,1,0:T(2,128)(2,1)S(1)}, u32[]{:S(2)}, u32[]{:S(2)}) async-start(bf16[8,2,2560]{2,1,0:T(2,128)(2,1)} %reshape.54429), calls=%async_computation | async-start | bytes 163840 | tf_op jit(solution)/shard_map/all_to_all | solution.py:108
  422.4 120.0 %all-to-all-start.1 = ((bf16[8,256,20,64]{1,3,2,0:T(8,128)(2,1)}), bf16[8,256,20,64]{1,3,2,0:T(8,128)(2,1)}, u32[]{:S(2)}, u32[]{:S(2)}) async-start(bf16[8,256,20,64]{1,3,2,0:T(8,128)(2,1)} %copy.5377), calls=%async_computation.1 | async-start | bytes 10485760 | tf_op jit(solution)/shard_map/all_to_all | solution.py:140
where the time goes:
time: 584 us; the launch traced here: 573 us
  other arithmetic  211 us (36%)
  local copies, waits for them, and re-layouts  130 us (22%)
  waiting for transfers between devices  105 us (18%)
  loops' own time  59.2 us (10%)
  matrix products  49 us (8%)
  starting transfers between devices  11.7 us (2%)
  blocking collectives  6.27 us (1%)
    while x2032, other arithmetic  179 us
    all_to_all x1, waiting for transfers between devices, body(): lax.all_to_all(shortened(spread), 'blk', split_axis=0, concat_axis=3, til...  97.8 us
    another operation x1, loops' own time, body(): blocks_out = lax.map(one_block, jnp.arange(block_count, dtype=jnp.int32))  59.2 us
    sqrt x1040, other arithmetic, recur_coef(): jnp.sqrt((4.0 * degree * degree - 1.0) / ((degree - m_column) * (degree +...  30 us
    another operation x16, local copies, waits for them, and re-layouts, legendre_rows(): return jnp.stack(stacked_rows, axis=1)  25.1 us
    transpose x2, local copies, waits for them, and re-layouts, body(): jnp.transpose(blocks_out, (1, 2, 0, 3))  19.7 us
    dot_general x16, matrix products, one_block(): jnp.einsum('qlr,qnr->qnl', legendre_tile, cycle_modes, preferred_element_...  17.9 us
    reshape x1, local copies, waits for them, and re-layouts, body(): split_piece = received.reshape(item_count, 2, maps_count, received.shape[3])  14.1 us
  transfers between devices with their start and end apart: 2, of which 2 were waited for; matrix products, arithmetic and copies ran while one was open for 3% of the time, Pallas kernels for 0%

commit v1 on v0

--- a/solution.py
+++ b/solution.py
@@ -1,8 +1,11 @@
+import functools
 import math
 
 import jax
 import jax.numpy as jnp
 from jax import lax
+from jax.experimental import pallas as pl
+from jax.experimental.pallas import tpu as pltpu
 from jax.sharding import PartitionSpec as P
 
 NSIDE = 8192
@@ -93,6 +96,207 @@
         value_newer = value_now
         prior_coef = present_coef
     return jnp.stack(stacked_rows, axis=1)
+
+
+STEP_LANES = 512
+KDIM = 256
+GAP = 8
+
+
+def spectra_kernel(
+    dims, starts_ref, z_ref, m_ref, base_ref, modes_ref, harm_ref, cross_ref,
+    p_ref, turned_ref, pieces_ref, kap_ref, leg_ref, acc_ref,
+):
+    blocks, cycles, maps, q_group, pad_maps, scale = dims
+    step = pl.program_id(0)
+    groups = STEP_LANES // KDIM
+    halves = STEP_LANES // 128
+    parts = 2 * maps
+    rows_out = q_group * pad_maps
+
+    @pl.when(step == 0)
+    def _():
+        m_row = m_ref[...]
+        piece = lax.broadcasted_iota(jnp.int32, (blocks, 256), 1) // 64
+
+        def setup(j, carry):
+            p_prev, q_prev = carry
+            degree = base_ref[...] + j.astype(jnp.float32)
+            num = 4.0 * degree * degree - 1.0
+            den = (degree - m_row) * (degree + m_row)
+            root = lax.rsqrt(num * den)
+            kappa = p_prev * p_prev
+            high = kappa.astype(jnp.bfloat16).astype(jnp.float32)
+            rest = kappa - high
+            mid = rest.astype(jnp.bfloat16).astype(jnp.float32)
+            low = rest - mid
+            pieces = jnp.where(piece == 0, high, jnp.where(piece == 1, mid, low))
+            pieces_ref[pl.ds(pl.multiple_of(j * blocks, blocks), blocks), :] = pieces.astype(
+                jnp.bfloat16
+            )
+            p_now = num * root * q_prev
+            q_now = den * root * p_prev
+            for half in range(blocks // 8):
+                p_ref[pl.ds(half * 8 * (LBLK + GAP) + j, 8, stride=LBLK + GAP), :] = p_now[
+                    half * 8 : half * 8 + 8, :128
+                ]
+            return p_now, q_now
+
+        one = jnp.ones((blocks, 256), jnp.float32)
+        lax.fori_loop(0, LBLK, setup, (one, one), unroll=4)
+        acc_ref[...] = jnp.zeros_like(acc_ref)
+
+        def turn(t, _):
+            turned_ref[t] = p_ref[pl.ds(pl.multiple_of(t * (LBLK + GAP), 8), LBLK), :].T
+            return 0
+
+        lax.fori_loop(0, blocks, turn, 0)
+
+    q_row = lax.broadcasted_iota(jnp.int32, (256, STEP_LANES), 0)
+    q_lane = lax.broadcasted_iota(jnp.int32, (256, STEP_LANES), 1) // cycles + step * (
+        STEP_LANES // cycles
+    )
+    spread = jnp.where((q_row % 64 == q_lane) & (q_row < 192), 1.0, 0.0).astype(jnp.bfloat16)
+
+    def widen(i, _):
+        rows = pl.ds(pl.multiple_of(i * 256, 256), 256)
+        kap_ref[rows, :] = jnp.dot(
+            pieces_ref[rows, :], spread, preferred_element_type=jnp.float32
+        ) * z_ref[...]
+        return 0
+
+    lax.fori_loop(0, blocks * LBLK // 256, widen, 0, unroll=2)
+
+    def recur(j, carry):
+        older, newer = carry
+        kap = kap_ref[pl.ds(pl.multiple_of(j * blocks, blocks), blocks), :]
+        now = kap * newer - older
+        for half in range(blocks // 8):
+            for g in range(halves):
+                leg_ref[g, pl.ds(half * 8 * (LBLK + GAP) + j, 8, stride=LBLK + GAP), :] = now[
+                    half * 8 : half * 8 + 8, g * 128 : g * 128 + 128
+                ]
+        return newer, now
+
+    lax.fori_loop(0, LBLK, recur, (starts_ref[0], starts_ref[1]), unroll=8)
+
+    rows_all = modes_ref.shape[1]
+    row = lax.broadcasted_iota(jnp.int32, (rows_all, KDIM), 0)
+    lane = lax.broadcasted_iota(jnp.int32, (rows_all, KDIM), 1)
+    row_q = jnp.where(row < rows_out, row // pad_maps, (row - rows_out) % q_group)
+    same_q = row_q == lane // cycles
+    cyc = lax.broadcasted_iota(jnp.int32, (cycles, KDIM), 0)
+    lane_c = lax.broadcasted_iota(jnp.int32, (cycles, KDIM), 1) % cycles
+    tile = jnp.where(cyc == lane_c, 1.0, 0.0).astype(jnp.bfloat16)
+    weights = []
+    for g in range(groups):
+        wide = jnp.dot(modes_ref[g], tile, preferred_element_type=jnp.float32)
+        weights.append(jnp.where(same_q, wide, 0.0).astype(jnp.bfloat16))
+
+    def project(t, _):
+        cols = pl.ds(pl.multiple_of(t * LBLK, LBLK), LBLK)
+        src = pl.ds(pl.multiple_of(t * (LBLK + GAP), 8), LBLK)
+        spectra_rows = []
+        for g in range(groups):
+            first = pl.multiple_of((step * groups + g) * q_group, 8)
+            p_rows = turned_ref[t, pl.ds(first, q_group), :] * scale
+            leg = jnp.concatenate(
+                [leg_ref[g * (KDIM // 128) + h, src, :] for h in range(KDIM // 128)], axis=1
+            ).astype(jnp.bfloat16)
+            out = lax.dot_general(
+                weights[g], leg, (((1,), (1,)), ((), ())), preferred_element_type=jnp.float32
+            )
+            direct = out[:rows_out].reshape(q_group, pad_maps, LBLK) * p_rows[:, None, :]
+            harm_ref[g * q_group : (g + 1) * q_group, :, cols] = direct[:, :parts].astype(
+                jnp.bfloat16
+            )
+            crossed = out[rows_out:].reshape(parts, q_group, LBLK) * p_rows[None]
+            spectra_rows.append(crossed.astype(jnp.bfloat16).astype(jnp.float32))
+        pair = 0
+        for i in range(maps):
+            for k in range(i, maps):
+                total = acc_ref[pair, :, cols]
+                for x in spectra_rows:
+                    total = total + x[i] * x[k] + x[maps + i] * x[maps + k]
+                acc_ref[pair, :, cols] = total
+                pair += 1
+        return 0
+
+    lax.fori_loop(0, blocks, project, 0)
+
+    @pl.when(step == pl.num_programs(0) - 1)
+    def _():
+        def finish(t, _):
+            cols = pl.ds(pl.multiple_of(t * LBLK, LBLK), LBLK)
+            cross_ref[:, cols] = jnp.sum(acc_ref[:, :, cols], axis=1)
+            return 0
+
+        lax.fori_loop(0, blocks, finish, 0)
+
+
+def project_blocks(legendre_starts, heights, m_float, first_l, modes, maps_count, cycle_scale):
+    local_cols, block_count, cycles = legendre_starts.shape[1:]
+    local_len = block_count * LBLK
+    q_group = KDIM // cycles
+    parts = 2 * maps_count
+    pad_maps = -(-parts // 8) * 8
+    pairs = maps_count * (maps_count + 1) // 2
+    base_l = first_l.astype(jnp.float32) + LBLK * jnp.arange(block_count, dtype=jnp.float32)
+    degree = base_l[None, :] - 1.0
+    m_col = m_float[:, None]
+    coef = jnp.sqrt((4.0 * degree * degree - 1.0) / ((degree - m_col) * (degree + m_col)))
+    starts = jnp.stack([legendre_starts[0] / coef[:, :, None], legendre_starts[1]])
+    starts = jnp.transpose(starts, (0, 2, 1, 3)).reshape(2, block_count, local_cols * cycles)
+    z_row = jnp.tile(heights, STEP_LANES // cycles)[None]
+    m_row = jnp.tile(m_float, 256 // local_cols)[None]
+    base = jnp.broadcast_to(base_l[:, None], (block_count, 256))
+    grouped = modes.reshape(local_cols // q_group, q_group, parts, cycles)
+    padded = jnp.pad(grouped, ((0, 0), (0, 0), (0, pad_maps - parts), (0, 0)))
+    ordered = jnp.concatenate(
+        [
+            padded.reshape(local_cols // q_group, q_group * pad_maps, cycles),
+            jnp.transpose(grouped, (0, 2, 1, 3)).reshape(
+                local_cols // q_group, parts * q_group, cycles
+            ),
+        ],
+        axis=1,
+    )
+    groups = STEP_LANES // KDIM
+    step_cols = groups * q_group
+    dims = (block_count, cycles, maps_count, q_group, pad_maps, cycle_scale)
+    whole = lambda shape: pl.BlockSpec(shape, lambda i: (0,) * len(shape))
+    return pl.pallas_call(
+        functools.partial(spectra_kernel, dims),
+        grid=(local_cols // step_cols,),
+        out_shape=(
+            jax.ShapeDtypeStruct((local_cols, parts, local_len), jnp.bfloat16),
+            jax.ShapeDtypeStruct((pairs, local_len), jnp.float32),
+        ),
+        in_specs=[
+            pl.BlockSpec((2, block_count, STEP_LANES), lambda i: (0, 0, i)),
+            whole((1, STEP_LANES)),
+            whole((1, 256)),
+            whole((block_count, 256)),
+            pl.BlockSpec((groups, ordered.shape[1], cycles), lambda i: (i, 0, 0)),
+        ],
+        out_specs=(
+            pl.BlockSpec((step_cols, parts, local_len), lambda i: (i, 0, 0)),
+            whole((pairs, local_len)),
+        ),
+        scratch_shapes=[
+            pltpu.VMEM((block_count * (LBLK + GAP), 128), jnp.float32),
+            pltpu.VMEM((block_count, 128, LBLK), jnp.float32),
+            pltpu.VMEM((local_len, 256), jnp.bfloat16),
+            pltpu.VMEM((local_len, STEP_LANES), jnp.float32),
+            pltpu.VMEM((STEP_LANES // 128, block_count * (LBLK + GAP), 128), jnp.float32),
+            pltpu.VMEM((pairs, 8, local_len), jnp.float32),
+        ],
+        compiler_params=pltpu.CompilerParams(vmem_limit_bytes=60 * 1024 * 1024),
+    )(starts, z_row, m_row, base, ordered)
+
+
+def kernel_fits(local_cols, cycles, block_count):
+    return cycles == 32 and local_cols == 64 and block_count % 8 == 0
 
 
 def body(sky_maps, cycle_number, legendre_starts):
@@ -117,6 +321,21 @@
     first_l = LSTART + lax.axis_index("map") * local_len
     cycle_scale = 1.0 / math.sqrt(cycle_modes.shape[-1])
 
+    if kernel_fits(local_cols, cycle_modes.shape[-1], block_count):
+        harmonics, cross = project_blocks(
+            legendre_starts, heights, m_float, first_l, cycle_modes, maps_count, cycle_scale
+        )
+        owned = lax.psum_scatter(cross, "blk", scatter_dimension=1, tiled=True)
+        pair_of = [[0] * maps_count for _ in range(maps_count)]
+        pair = 0
+        for i in range(maps_count):
+            for k in range(i, maps_count):
+                pair_of[i][k] = pair_of[k][i] = pair
+                pair += 1
+        rows = [owned[pair_of[i][k]] for i in range(maps_count) for k in range(maps_count)]
+        spectra = jnp.stack(rows).reshape(maps_count, maps_count, -1) / (MGRP * RES)
+        return (harmonics, spectra[None])
+
     def one_block(block_index):
         start_pair = lax.dynamic_index_in_dim(legendre_starts, block_index, 2, keepdims=False)
         legendre_tile = legendre_rows(

time: 584 us -> 180 us (0.31); the launches traced: 573 us -> 179 us
  other arithmetic: 211 us -> 1.72 us
  local copies, waits for them, and re-layouts: 130 us -> 35.1 us
  loops' own time: 59.2 us -> 0 us
  waiting for transfers between devices: 105 us -> 56 us
  Pallas kernels: 0 us -> 37.1 us
  matrix products: 49 us -> 21.4 us
  between operations: 1.68 us -> 14.9 us
    while x2032 -> x0, other arithmetic: 179 us -> none
    all_to_all x1 -> x0, waiting for transfers between devices: 97.8 us -> none  [body(): lax.all_to_all(shortened(spread), 'blk', split_axis=0, concat_axis=3, til...]
    another operation x1 -> x0, loops' own time: 59.2 us -> none  [body(): blocks_out = lax.map(one_block, jnp.arange(block_count, dtype=jnp.int32))]
    reduce_scatter x0 -> x1, waiting for transfers between devices: none -> 52.4 us  [body(): owned = lax.psum_scatter(cross, 'blk', scatter_dimension=1, tiled=True)]
    pallas_call x0 -> x1, Pallas kernels: none -> 37.1 us  [project_blocks(): pl.pallas_call(functools.partial(spectra_kernel, dims), grid=(local_cols...]
    another operation x18 -> x6, local copies, waits for them, and re-layouts: 33.7 us -> 2.03 us  [the longest x2 0.67 us: project_blocks(): z_row = jnp.tile(heights, STEP_LANES // cycles)[None]]
    sqrt x1040 -> x1, other arithmetic: 30 us -> 0.08 us  [project_blocks(): jnp.sqrt((4.0 * degree * degree - 1.0) / ((degree - m_col) * (degree + m_...]
    dot_general x17 -> x0, matrix products: 27.6 us -> none  [the longest x16 17.9 us: one_block(): jnp.einsum('qlr,qnr->qnl', legendre_tile, cycle_modes, preferred_element_...]
  transfers between devices with their start and end apart: 2 -> 2, of which waited for: 2 -> 2; matrix products, arithmetic and copies ran while one was open for 3% -> 6% of each run, Pallas kernels for 0% -> 0%
where the time goes in v1:
time: 180 us; the launch traced here: 179 us
  waiting for transfers between devices  56 us (31%)
  Pallas kernels  37.1 us (21%)
  local copies, waits for them, and re-layouts  35.1 us (20%)
  matrix products  21.4 us (12%)
  between operations  14.9 us (8%)
  starting transfers between devices  6.51 us (4%)
  blocking collectives  6.27 us (3%)
    reduce_scatter x1, waiting for transfers between devices, body(): owned = lax.psum_scatter(cross, 'blk', scatter_dimension=1, tiled=True)  52.4 us
    pallas_call x1, Pallas kernels, project_blocks(): pl.pallas_call(functools.partial(spectra_kernel, dims), grid=(local_cols...  37.1 us
    unnamed x9, local copies, waits for them, and re-layouts  14.6 us
    slice x12, local copies, waits for them, and re-layouts, body(): owned[pair_of[i][k]]  9.2 us
    all_to_all x1, starting transfers between devices, body(): lax.all_to_all(grouped, 'blk', split_axis=4, concat_axis=0, tiled=True)  6.29 us
    all_gather x1, blocking collectives, body(): grouped = lax.all_gather(local_modes, 'map', axis=0, tiled=True)  6.27 us
    dot_general x1, matrix products, cycle_transform(): jnp.einsum('rnjk,cjk->rnck', part_im, twiddle_im, preferred_element_type=...  5.28 us
    dot_general x1, matrix products, cycle_transform(): jnp.einsum('rnjk,cjk->rnck', part_re, twiddle_im, preferred_element_type=...  5.26 us
  transfers between devices with their start and end apart: 2, of which 2 were waited for; matrix products, arithmetic and copies ran while one was open for 6% of the time, Pallas kernels for 0%

profile of v1, /device:TPU:0, one launch (start us, length us, event | category | flops | bytes accessed | tf_op | source)
XLA Modules:
  0.0 178.9 jit_solution(14687976962065043017)
XLA Ops:
  7.2 1.2 dynamic_slice.3
  9.1 0.3 negate_convert_fusion.3
  9.4 0.1 iota_add_fusion
  9.4 0.1 fusion.32
  9.6 0.1 copy.69
  9.7 0.1 copy.73
  9.8 1.5 copy.89
  11.3 0.5 fusion
  11.7 0.1 slice_bitcast_fusion
  11.8 0.1 copy.70
  12.0 5.2 %fusion.3 = f32[128,4,10]{2,1,0:T(4,128)S(1)} fusion(bf16[10,256,128]{1,2,0:T(8,128)(2,1)S(1)} %get-tuple-element.18, s32[4,128]{0,1:T(8,128)S(1)} %copy.70), kind=kOutput, calls=%fused_computation.6 | convolution fusion | flops 4587520 | bytes 677888 | tf_op jit(solution)/shard_map/rnjk,cjk->rnck/dot_general | solution.py:63
  17.1 5.2 %fusion.7 = f32[128,4,10]{2,1,0:T(4,128)S(1)} fusion(bf16[10,256,128]{1,2,0:T(8,128)(2,1)S(1)} %get-tuple-element.19, s32[4,128]{0,1:T(8,128)S(1)} %copy.70), kind=kOutput, calls=%fused_computation.10 | convolution fusion | flops 4587520 | bytes 677888 | tf_op jit(solution)/shard_map/rnjk,cjk->rnck/dot_general | solution.py:60
  22.3 5.3 %fusion.1 = f32[1,10,4,128]{1,2,3,0:T(4,128)S(1)} fusion(f32[128,4,10]{2,1,0:T(4,128)S(1)} %fusion.3, bf16[10,256,128]{1,2,0:T(8,128)(2,1)S(1)} %get-tuple-element.19, s32[4,128]{0,1:T(8,128)S(1)} %copy.70), kind=kOutput, calls=%fused_computation.3 | convolution fusion | flops 4723712 | bytes 698368 | tf_op jit(solution)/shard_map/rnjk,cjk->rnck/dot_general | solution.py:65
  27.6 5.3 %fusion.13 = (bf16[1,1,10,4,128]{2,3,4,1,0:T(4,128)(2,1)S(1)}, bf16[1,1,10,4,128]{2,3,4,1,0:T(4,128)(2,1)S(1)}) fusion(f32[1,10,4,128]{1,2,3,0:T(4,128)S(1)} %fusion.1, f32[4,128]{0,1:T(8,128)S(1)} %copy.73, f32[4,128]{0,1:T(8,128)S(1)} %copy.69, f32[128,4,10]{2,1,0:T(4,128)S(1)} %fusion.7, bf16[10,256,128]{1,2,0:T(8,128)(2,1)S(1)} %get-tuple-element.18, ...), kind=kOutput, calls=%fused_computation.29 | convolution fusion | flops 4774912 | bytes 722944 | tf_op jit(solution)/shard_map/rnjk,cjk->rnck/dot_general | solution.py:62
  32.8 0.0 copy-start
  32.8 0.1 copy.76
  33.0 0.1 copy.77
  33.1 6.3 %all_gather.3 = bf16[4,2,10,4,128]{4,3,2,1,0:T(4,128)(2,1)S(1)} all-gather(bf16[1,2,10,4,128]{4,3,2,1,0:T(4,128)(2,1)S(1)} %pad_maximum_fusion.1), channel_id=1, replica_groups=mesh['blk'=8,'map'=4] {'map'}, dimensions={0}, use_global_device_ids=true | all-gather | bytes 102400 | tf_op jit(solution)/shard_map/all_gather | solution.py:311
  39.4 1.0 copy.78
  40.4 2.5 %reshape.366 = bf16[8,2,2560]{2,1,0:T(2,128)(2,1)} reshape(bf16[128,4,2,4,10]{4,3,2,1,0:T(4,128)(2,1)S(1)} %bitcast.49) | data formatting | bytes 163840
  42.8 6.3 %all-to-all-start = ((bf16[8,2,2560]{2,1,0:T(2,128)(2,1)}), bf16[8,2,2560]{2,1,0:T(2,128)(2,1)S(1)}, u32[]{:S(2)}, u32[]{:S(2)}) async-start(bf16[8,2,2560]{2,1,0:T(2,128)(2,1)} %reshape.366), calls=%async_computation | async-start | bytes 163840 | tf_op jit(solution)/shard_map/all_to_all | solution.py:312
  49.1 0.2 reduce-scatter.2.cloned.1.call-start
  49.4 0.1 divide_sqrt_fusion
  49.5 0.0 copy-done
  49.6 0.0 copy-start.1
  49.6 0.4 copy.68
  50.0 1.2 reshape.359.starts_ref
  51.2 0.7 broadcast_in_dim_tile.7.m_ref
  51.8 0.0 copy-done.1
  51.8 0.7 broadcast_in_dim_tile.6.z_ref
  52.5 3.6 %all-to-all-done = bf16[8,2,2560]{2,1,0:T(2,128)(2,1)S(1)} async-done(((bf16[8,2,2560]{2,1,0:T(2,128)(2,1)}), bf16[8,2,2560]{2,1,0:T(2,128)(2,1)S(1)}, u32[]{:S(2)}, u32[]{:S(2)}) %all-to-all-start) | async-done | bytes 81952 | tf_op jit(solution)/shard_map/all_to_all | solution.py:312
  56.1 2.5 %reshape.367 = bf16[128,4,2,4,10]{4,3,2,1,0:T(4,128)(2,1)S(1)} reshape(bf16[8,2,2560]{2,1,0:T(2,128)(2,1)S(1)} %all-to-all-done) | data formatting | bytes 163840
  58.6 3.0 %copy.79 = bf16[4,2,10,4,8,16]{5,0,4,3,2,1:T(4,128)(2,1)S(1)} copy(bf16[4,2,10,4,8,16]{2,3,1,0,5,4:T(4,128)(2,1)S(1)} %bitcast.50) | data formatting | bytes 163840 | tf_op jit(solution)/shard_map/all_to_all | solution.py:312
  61.6 0.3 copy.80
  62.0 0.2 copy.88
  62.2 0.1 copy.101
  62.3 0.1 pad.4.clone
  62.4 1.0 pad_maximum_fusion.modes_ref
  63.4 0.7 broadcast_in_dim.2.base_ref
  64.0 37.1 %shard_map.50 = (bf16[64,20,2048]{2,1,0:T(8,128)(2,1)}, f32[55,2048]{1,0:T(8,128)}) custom-call(f32[2,16,2048]{2,1,0:T(8,128)} %reshape.359.starts_ref, f32[1,512]{1,0:T(1,128)} %broadcast_in_dim_tile.6.z_ref, f32[1,256]{1,0:T(1,128)} %broadcast_in_dim_tile.7.m_ref, f32[16,256]{1,0:T(8,128)} %broadcast_in_dim.2.base_ref, ...), custom_call_target="tpu_custom_call" | custom-call | tf_op jit(solution)/shard_map/pallas_call | solution.py:268
  101.1 0.0 reduce-scatter.2.cloned.1.call-update
  101.1 8.0 %copy.84 = bf16[64,20,2048]{2,0,1:T(8,128)(2,1)} copy(bf16[64,20,2048]{2,1,0:T(8,128)(2,1)} %get-tuple-element.16) | data formatting | bytes 10485760
  109.1 52.4 %reduce-scatter.2.cloned.1.call-done = f32[55,256]{1,0:T(8,128)} async-done(((f32[55,2048]{1,0:T(8,128)}), f32[55,256]{1,0:T(8,128)}) %reduce-scatter.2.cloned.1.call-update) | async-done | bytes 56336 | tf_op jit(solution)/shard_map/reduce_scatter | solution.py:328
  161.5 0.9 fusion.51
  162.4 1.0 fusion.52
  163.4 0.7 slice.290
  164.1 0.7 slice.292
  164.9 0.7 slice.295
  165.6 0.7 slice.299
  166.3 0.7 slice.304
  167.0 0.7 slice.310
  167.7 0.8 fusion.53
  168.5 0.8 fusion.50
  169.3 0.7 slice.317
  170.0 0.7 slice.325
  170.7 0.6 stack.21
  171.3 0.7 div.60
  (11 shorter events, 0.2 us)
Async XLA Ops:
  32.8 16.6 %copy-start = (f32[2,64,16,32]{1,3,2,0:T(8,128)S(1)}, f32[2,64,16,32]{1,3,2,0:T(8,128)}, u32[]{:S(2)}) copy-start(f32[2,64,16,32]{1,3,2,0:T(8,128)} %param.5) | copy-start | bytes 786436
  42.8 13.3 %all-to-all-start = ((bf16[8,2,2560]{2,1,0:T(2,128)(2,1)}), bf16[8,2,2560]{2,1,0:T(2,128)(2,1)S(1)}, u32[]{:S(2)}, u32[]{:S(2)}) async-start(bf16[8,2,2560]{2,1,0:T(2,128)(2,1)} %reshape.366), calls=%async_computation | async-start | bytes 163840 | tf_op jit(solution)/shard_map/all_to_all | solution.py:312
  49.1 112.4 %reduce-scatter.2.cloned.1.call-start = ((), (), s32[]{:S(2)}) async-start(), calls=%async_computation.2 | async-start | bytes 516096 | tf_op jit(solution)/shard_map/reduce_scatter | solution.py:328
  49.6 2.2 %copy-start.1 = (s32[32]{0:T(128)S(1)}, s32[32]{0:T(128)}, u32[]{:S(2)}) copy-start(s32[32]{0:T(128)} %param.4) | copy-start | bytes 388
Sparse Core Ops, SparseCore 0:
  101.2 60.1 reduce-scatter.1

commit v2 on v1

--- a/solution.py
+++ b/solution.py
@@ -3,6 +3,7 @@
 
 import jax
 import jax.numpy as jnp
+import numpy as np
 from jax import lax
 from jax.experimental import pallas as pl
 from jax.experimental.pallas import tpu as pltpu
@@ -107,12 +108,11 @@
     dims, starts_ref, z_ref, m_ref, base_ref, modes_ref, harm_ref, cross_ref,
     p_ref, turned_ref, pieces_ref, kap_ref, leg_ref, acc_ref,
 ):
-    blocks, cycles, maps, q_group, pad_maps, scale = dims
+    blocks, cycles, maps, q_group, scale = dims
     step = pl.program_id(0)
     groups = STEP_LANES // KDIM
     halves = STEP_LANES // 128
     parts = 2 * maps
-    rows_out = q_group * pad_maps
 
     @pl.when(step == 0)
     def _():
@@ -180,17 +180,28 @@
 
     lax.fori_loop(0, LBLK, recur, (starts_ref[0], starts_ref[1]), unroll=8)
 
-    rows_all = modes_ref.shape[1]
+    rows_all = parts * q_group
+    row = lax.broadcasted_iota(jnp.int32, (rows_all, 128), 0)
+    lane = lax.broadcasted_iota(jnp.int32, (rows_all, 128), 1)
+    picked = (row % MGRP) * parts + row // q_group == lane
     row = lax.broadcasted_iota(jnp.int32, (rows_all, KDIM), 0)
     lane = lax.broadcasted_iota(jnp.int32, (rows_all, KDIM), 1)
-    row_q = jnp.where(row < rows_out, row // pad_maps, (row - rows_out) % q_group)
-    same_q = row_q == lane // cycles
+    same_q = row % q_group == lane // cycles
     cyc = lax.broadcasted_iota(jnp.int32, (cycles, KDIM), 0)
     lane_c = lax.broadcasted_iota(jnp.int32, (cycles, KDIM), 1) % cycles
     tile = jnp.where(cyc == lane_c, 1.0, 0.0).astype(jnp.bfloat16)
+    row_k = lax.broadcasted_iota(jnp.int32, (rows_all, 128), 0) % q_group // MGRP
+    per_group = q_group // MGRP
     weights = []
     for g in range(groups):
-        wide = jnp.dot(modes_ref[g], tile, preferred_element_type=jnp.float32)
+        narrow = jnp.zeros((rows_all, cycles), jnp.float32)
+        for k in range(per_group):
+            pick = jnp.where(picked & (row_k == k), 1.0, 0.0).astype(jnp.bfloat16)
+            narrow = narrow + lax.dot_general(
+                pick, modes_ref[g * per_group + k], (((1,), (1,)), ((), ())),
+                preferred_element_type=jnp.float32,
+            )
+        wide = jnp.dot(narrow.astype(jnp.bfloat16), tile, preferred_element_type=jnp.float32)
         weights.append(jnp.where(same_q, wide, 0.0).astype(jnp.bfloat16))
 
     def project(t, _):
@@ -206,12 +217,10 @@
             out = lax.dot_general(
                 weights[g], leg, (((1,), (1,)), ((), ())), preferred_element_type=jnp.float32
             )
-            direct = out[:rows_out].reshape(q_group, pad_maps, LBLK) * p_rows[:, None, :]
-            harm_ref[g * q_group : (g + 1) * q_group, :, cols] = direct[:, :parts].astype(
-                jnp.bfloat16
-            )
-            crossed = out[rows_out:].reshape(parts, q_group, LBLK) * p_rows[None]
-            spectra_rows.append(crossed.astype(jnp.bfloat16).astype(jnp.float32))
+            crossed = out.reshape(parts, q_group, LBLK) * p_rows[None]
+            crossed = crossed.astype(jnp.bfloat16)
+            harm_ref[:, g * q_group : (g + 1) * q_group, cols] = crossed
+            spectra_rows.append(crossed.astype(jnp.float32))
         pair = 0
         for i in range(maps):
             for k in range(i, maps):
@@ -226,20 +235,24 @@
 
     @pl.when(step == pl.num_programs(0) - 1)
     def _():
-        def finish(t, _):
-            cols = pl.ds(pl.multiple_of(t * LBLK, LBLK), LBLK)
-            cross_ref[:, cols] = jnp.sum(acc_ref[:, :, cols], axis=1)
+        share = cross_ref.shape[2]
+
+        def finish(d, _):
+            for part in range(share // LBLK):
+                cols = pl.ds(pl.multiple_of(d * share + part * LBLK, LBLK), LBLK)
+                cross_ref[d, : acc_ref.shape[0], part * LBLK : (part + 1) * LBLK] = jnp.sum(
+                    acc_ref[:, :, cols], axis=1
+                ).astype(cross_ref.dtype)
             return 0
 
-        lax.fori_loop(0, blocks, finish, 0)
-
-
-def project_blocks(legendre_starts, heights, m_float, first_l, modes, maps_count, cycle_scale):
+        lax.fori_loop(0, cross_ref.shape[0], finish, 0)
+
+
+def project_blocks(legendre_starts, heights, m_float, first_l, modes, maps_count, cycle_scale, blk_total):
     local_cols, block_count, cycles = legendre_starts.shape[1:]
     local_len = block_count * LBLK
     q_group = KDIM // cycles
     parts = 2 * maps_count
-    pad_maps = -(-parts // 8) * 8
     pairs = maps_count * (maps_count + 1) // 2
     base_l = first_l.astype(jnp.float32) + LBLK * jnp.arange(block_count, dtype=jnp.float32)
     degree = base_l[None, :] - 1.0
@@ -250,38 +263,29 @@
     z_row = jnp.tile(heights, STEP_LANES // cycles)[None]
     m_row = jnp.tile(m_float, 256 // local_cols)[None]
     base = jnp.broadcast_to(base_l[:, None], (block_count, 256))
-    grouped = modes.reshape(local_cols // q_group, q_group, parts, cycles)
-    padded = jnp.pad(grouped, ((0, 0), (0, 0), (0, pad_maps - parts), (0, 0)))
-    ordered = jnp.concatenate(
-        [
-            padded.reshape(local_cols // q_group, q_group * pad_maps, cycles),
-            jnp.transpose(grouped, (0, 2, 1, 3)).reshape(
-                local_cols // q_group, parts * q_group, cycles
-            ),
-        ],
-        axis=1,
-    )
     groups = STEP_LANES // KDIM
     step_cols = groups * q_group
-    dims = (block_count, cycles, maps_count, q_group, pad_maps, cycle_scale)
+    dims = (block_count, cycles, maps_count, q_group, cycle_scale)
+    pair_rows = -(-pairs // 16) * 16
+    share = local_len // blk_total
     whole = lambda shape: pl.BlockSpec(shape, lambda i: (0,) * len(shape))
     return pl.pallas_call(
         functools.partial(spectra_kernel, dims),
         grid=(local_cols // step_cols,),
         out_shape=(
-            jax.ShapeDtypeStruct((local_cols, parts, local_len), jnp.bfloat16),
-            jax.ShapeDtypeStruct((pairs, local_len), jnp.float32),
+            jax.ShapeDtypeStruct((parts, local_cols, local_len), jnp.bfloat16),
+            jax.ShapeDtypeStruct((blk_total, pair_rows, share), jnp.bfloat16),
         ),
         in_specs=[
             pl.BlockSpec((2, block_count, STEP_LANES), lambda i: (0, 0, i)),
             whole((1, STEP_LANES)),
             whole((1, 256)),
             whole((block_count, 256)),
-            pl.BlockSpec((groups, ordered.shape[1], cycles), lambda i: (i, 0, 0)),
+            pl.BlockSpec((step_cols // MGRP, cycles, 128), lambda i: (i, 0, 0)),
         ],
         out_specs=(
-            pl.BlockSpec((step_cols, parts, local_len), lambda i: (i, 0, 0)),
-            whole((pairs, local_len)),
+            pl.BlockSpec((parts, step_cols, local_len), lambda i: (0, i, 0)),
+            whole((blk_total, pair_rows, share)),
         ),
         scratch_shapes=[
             pltpu.VMEM((block_count * (LBLK + GAP), 128), jnp.float32),
@@ -292,18 +296,202 @@
             pltpu.VMEM((pairs, 8, local_len), jnp.float32),
         ],
         compiler_params=pltpu.CompilerParams(vmem_limit_bytes=60 * 1024 * 1024),
-    )(starts, z_row, m_row, base, ordered)
-
-
-def kernel_fits(local_cols, cycles, block_count):
-    return cycles == 32 and local_cols == 64 and block_count % 8 == 0
+    )(starts, z_row, m_row, base, modes)
+
+
+def modes_kernel(totals, sky_ref, first_ref, wr_ref, wi_ref, phase_ref, out_ref,
+                 rows_ref, turned_ref, held_ref, send_sem, recv_sem):
+    blk_total, map_total, factor = totals
+    maps = sky_ref.shape[0]
+    count = blk_total * map_total
+    me_blk, me_map = lax.axis_index("blk"), lax.axis_index("map")
+    me = me_blk * map_total + me_map
+    share = RES // blk_total
+    barrier = pltpu.get_barrier_semaphore()
+    for i in range(1, count):
+        peer = lax.rem(me + i, count)
+        pl.semaphore_signal(
+            barrier, inc=1,
+            device_id={"blk": peer // map_total, "map": lax.rem(peer, map_total)},
+            device_id_type=pl.DeviceIdType.MESH,
+        )
+    rows_ref[...] = jnp.zeros_like(rows_ref)
+    first = first_ref[...]
+    for n in range(maps):
+        section = lax.dot_general(
+            sky_ref[n], first, (((0,), (0,)), ((), ())), preferred_element_type=jnp.float32
+        )
+        section = section.astype(jnp.bfloat16).astype(jnp.float32)
+        part_re, part_im = section[:, :RES], section[:, RES:]
+        for c in range(MGRP):
+            wave_re = wr_ref[c].astype(jnp.float32)
+            wave_im = wi_ref[c].astype(jnp.float32)
+            real = jnp.sum(wave_re * part_re - wave_im * part_im, axis=0, keepdims=True)
+            imag = jnp.sum(wave_re * part_im + wave_im * part_re, axis=0, keepdims=True)
+            cos, sin = phase_ref[c : c + 1], phase_ref[MGRP + c : MGRP + c + 1]
+            row = c * 2 * maps + n
+            rows_ref[row : row + 1, :] = factor * (cos * real + sin * imag)
+            rows_ref[row + maps : row + maps + 1, :] = factor * (cos * imag - sin * real)
+    turned_ref[...] = rows_ref[...].T.astype(jnp.bfloat16)
+    pl.semaphore_wait(barrier, count - 1)
+
+    def copy_to(peer, source):
+        target_blk = peer // map_total
+        return pltpu.make_async_remote_copy(
+            src_ref=turned_ref.at[pl.ds(pl.multiple_of(target_blk * share, share), share)],
+            dst_ref=held_ref.at[source],
+            send_sem=send_sem.at[peer],
+            recv_sem=recv_sem.at[source],
+            device_id={"blk": target_blk, "map": lax.rem(peer, map_total)},
+            device_id_type=pl.DeviceIdType.MESH,
+        )
+
+    for i in range(1, count):
+        copy_to(lax.rem(me + i, count), me).start()
+    held_ref[me] = turned_ref[pl.ds(pl.multiple_of(me_blk * share, share), share), :]
+    for i in range(1, count):
+        peer = lax.rem(me + i, count)
+        copy_to(peer, peer).wait_recv()
+    for i in range(1, count):
+        copy_to(lax.rem(me + i, count), me).wait_send()
+    gathered = held_ref[...].astype(jnp.float32)
+    out_ref[...] = jnp.swapaxes(gathered, 0, 1).astype(jnp.bfloat16)
+
+
+def exchange_modes(sky_maps, parity, blk_total, map_total):
+    _, maps, cycle_len = sky_maps.shape
+    first_table, wave_re, wave_im = constant_tables(cycle_len)
+    m_value = MSTART + np.arange(MGRP)[:, None] * RES + np.arange(RES)[None, :]
+    m_value = jnp.asarray(m_value, jnp.int32)
+    angle = math.pi / cycle_len * (m_value * parity[0] % (2 * cycle_len)).astype(jnp.float32)
+    phase = jnp.concatenate([jnp.cos(angle), jnp.sin(angle)], axis=0)
+    count = blk_total * map_total
+    return pl.pallas_call(
+        functools.partial(modes_kernel, (blk_total, map_total, 1.0 / math.sqrt(cycle_len))),
+        out_shape=jax.ShapeDtypeStruct((RES // blk_total, count, 128), jnp.bfloat16),
+        in_specs=[pl.BlockSpec(memory_space=pltpu.VMEM)] * 5,
+        out_specs=pl.BlockSpec(memory_space=pltpu.VMEM),
+        scratch_shapes=[
+            pltpu.VMEM((128, RES), jnp.float32),
+            pltpu.VMEM((RES, 128), jnp.bfloat16),
+            pltpu.VMEM((count, RES // blk_total, 128), jnp.bfloat16),
+            pltpu.SemaphoreType.DMA((count,)),
+            pltpu.SemaphoreType.DMA((count,)),
+        ],
+        compiler_params=pltpu.CompilerParams(collective_id=0, has_side_effects=True),
+    )(sky_maps.reshape(maps, RES, cycle_len // RES), first_table, wave_re, wave_im, phase)
+
+
+def constant_tables(cycle_len):
+    low_len = cycle_len // RES
+    residue = np.arange(RES)
+    angle = np.float32(2.0 * math.pi / RES) * (
+        residue[:, None] * residue[None, :] % RES
+    ).astype(np.float32)
+    first = np.concatenate([np.cos(angle), -np.sin(angle)], axis=1)
+    m_value = MSTART + RES * np.arange(MGRP)[:, None, None] + residue[None, None, :]
+    turn = m_value * np.arange(low_len)[None, :, None] % cycle_len
+    angle = np.float32(2.0 * math.pi / cycle_len) * turn.astype(np.float32)
+    short = lambda table: jnp.asarray(table.astype(jnp.bfloat16))
+    return short(first), short(np.cos(angle)), short(-np.sin(angle))
+
+
+def total_kernel(blk_total, maps, part_ref, out_ref, held_ref, send_sem, recv_sem):
+    me = lax.axis_index("blk")
+    barrier = pltpu.get_barrier_semaphore()
+    for i in range(1, blk_total):
+        pl.semaphore_signal(
+            barrier, inc=1, device_id={"blk": lax.rem(me + i, blk_total)},
+            device_id_type=pl.DeviceIdType.MESH,
+        )
+    pl.semaphore_wait(barrier, blk_total - 1)
+
+    def copy_to(peer, source):
+        return pltpu.make_async_remote_copy(
+            src_ref=part_ref.at[peer],
+            dst_ref=held_ref.at[source],
+            send_sem=send_sem.at[peer],
+            recv_sem=recv_sem.at[source],
+            device_id={"blk": peer},
+            device_id_type=pl.DeviceIdType.MESH,
+        )
+
+    order = [lax.rem(me + i, blk_total) for i in range(1, blk_total)]
+    for peer in order:
+        copy_to(peer, me).start()
+    total = part_ref[me].astype(jnp.float32)
+    for peer in order:
+        copy_to(peer, peer).wait_recv()
+        total = total + held_ref[peer].astype(jnp.float32)
+    total = total * (1.0 / (MGRP * RES))
+    pair = 0
+    for i in range(maps):
+        for k in range(i, maps):
+            out_ref[i, k : k + 1, :] = total[pair : pair + 1]
+            if k > i:
+                out_ref[k, i : i + 1, :] = total[pair : pair + 1]
+            pair += 1
+    for peer in order:
+        copy_to(peer, me).wait_send()
+
+
+def total_cross(cross, maps):
+    blk_total, pair_rows, share = cross.shape
+    return pl.pallas_call(
+        functools.partial(total_kernel, blk_total, maps),
+        out_shape=jax.ShapeDtypeStruct((maps, maps, share), jnp.float32),
+        in_specs=[pl.BlockSpec(memory_space=pltpu.VMEM)],
+        out_specs=pl.BlockSpec(memory_space=pltpu.VMEM),
+        scratch_shapes=[
+            pltpu.VMEM(cross.shape, cross.dtype),
+            pltpu.SemaphoreType.DMA((blk_total,)),
+            pltpu.SemaphoreType.DMA((blk_total,)),
+        ],
+        compiler_params=pltpu.CompilerParams(collective_id=1, has_side_effects=True),
+    )(cross)
+
+
+def kernel_fits(own_cycles, blk_total, cycles, maps_count, block_count):
+    local_cols = MGRP * RES // blk_total
+    return (
+        own_cycles == 1
+        and local_cols == 64
+        and KDIM % cycles == 0
+        and KDIM // cycles == 8
+        and 2 * maps_count * MGRP <= 128
+        and block_count % 8 == 0
+        and block_count % blk_total == 0
+    )
+
+
+def fast_body(sky_maps, cycle_number, legendre_starts):
+    _, maps_count, _ = sky_maps.shape
+    map_total = lax.axis_size("map")
+    blk_total = lax.axis_size("blk")
+    row = lax.axis_index("blk") * map_total + lax.axis_index("map")
+    parity = (lax.dynamic_slice_in_dim(cycle_number, row, 1) - NSIDE + 1) % 2
+    modes = exchange_modes(sky_maps, parity, blk_total, map_total)
+    heights = cycle_height(cycle_number)
+    local_cols, block_count, cycles = legendre_starts.shape[1:]
+    column = lax.axis_index("blk") * local_cols + jnp.arange(local_cols, dtype=jnp.int32)
+    m_float = (MSTART + RES * (column % MGRP) + column // MGRP).astype(jnp.float32)
+    first_l = LSTART + lax.axis_index("map") * block_count * LBLK
+    cycle_scale = 1.0 / math.sqrt(cycles)
+    harmonics, cross = project_blocks(
+        legendre_starts, heights, m_float, first_l, modes, maps_count, cycle_scale, blk_total
+    )
+    spectra = total_cross(cross, maps_count)
+    return (jnp.transpose(harmonics, (1, 0, 2)), spectra[None])
 
 
 def body(sky_maps, cycle_number, legendre_starts):
     own_cycles, maps_count, cycle_len = sky_maps.shape
-    tables = dft_tables(cycle_len)
     map_total = lax.axis_size("map")
     blk_total = lax.axis_size("blk")
+    cycles, block_count = cycle_number.shape[0], legendre_starts.shape[2]
+    if kernel_fits(own_cycles, blk_total, cycles, maps_count, block_count):
+        return fast_body(sky_maps, cycle_number, legendre_starts)
+    tables = dft_tables(cycle_len)
     first_row = (lax.axis_index("blk") * map_total + lax.axis_index("map")) * own_cycles
     own_numbers = lax.dynamic_slice_in_dim(cycle_number, first_row, own_cycles)
     parity = (own_numbers - NSIDE + 1) % 2
@@ -321,21 +509,6 @@
     first_l = LSTART + lax.axis_index("map") * local_len
     cycle_scale = 1.0 / math.sqrt(cycle_modes.shape[-1])
 
-    if kernel_fits(local_cols, cycle_modes.shape[-1], block_count):
-        harmonics, cross = project_blocks(
-            legendre_starts, heights, m_float, first_l, cycle_modes, maps_count, cycle_scale
-        )
-        owned = lax.psum_scatter(cross, "blk", scatter_dimension=1, tiled=True)
-        pair_of = [[0] * maps_count for _ in range(maps_count)]
-        pair = 0
-        for i in range(maps_count):
-            for k in range(i, maps_count):
-                pair_of[i][k] = pair_of[k][i] = pair
-                pair += 1
-        rows = [owned[pair_of[i][k]] for i in range(maps_count) for k in range(maps_count)]
-        spectra = jnp.stack(rows).reshape(maps_count, maps_count, -1) / (MGRP * RES)
-        return (harmonics, spectra[None])
-
     def one_block(block_index):
         start_pair = lax.dynamic_index_in_dim(legendre_starts, block_index, 2, keepdims=False)
         legendre_tile = legendre_rows(

time: 180 us -> 71.1 us (0.39)
  waiting for transfers between devices: 56 us -> 0 us
  local copies, waits for them, and re-layouts: 35.1 us -> 7.63 us
  Pallas kernels: 37.1 us -> 58.6 us
  matrix products: 21.4 us -> 0 us
  between operations: 14.9 us -> 1.39 us
  starting transfers between devices: 6.51 us -> 0 us
  blocking collectives: 6.27 us -> 0 us
    reduce_scatter x1 -> x0, waiting for transfers between devices: 52.4 us -> none  [body(): owned = lax.psum_scatter(cross, 'blk', scatter_dimension=1, tiled=True)]
    pallas_call x0 -> x2, Pallas kernels: none -> 24.5 us  [the longest x1 13.6 us: exchange_modes(): pl.pallas_call(functools.partial(modes_kernel, (blk_total, map_total, 1.0...]
    dot_general x5 -> x0, matrix products: 21.4 us -> none  [the longest x1 5.28 us: cycle_transform(): jnp.einsum('rnjk,cjk->rnck', part_im, twiddle_im, preferred_element_type=...]
    unnamed x9 -> x4, local copies, waits for them, and re-layouts: 14.6 us -> 1.89 us
    slice x12 -> x0, local copies, waits for them, and re-layouts: 9.2 us -> none  [body(): owned[pair_of[i][k]]]
    all_to_all x1 -> x0, starting transfers between devices: 6.29 us -> none  [body(): lax.all_to_all(grouped, 'blk', split_axis=4, concat_axis=0, tiled=True)]
    all_gather x1 -> x0, blocking collectives: 6.27 us -> none  [body(): grouped = lax.all_gather(local_modes, 'map', axis=0, tiled=True)]
    all_to_all x1 -> x0, waiting for transfers between devices: 3.62 us -> none  [body(): lax.all_to_all(grouped, 'blk', split_axis=4, concat_axis=0, tiled=True)]
  transfers between devices with their start and end apart: 2 -> 0, of which waited for: 2 -> 0; matrix products, arithmetic and copies ran while one was open for 6% -> 0% of each run, Pallas kernels for 0% -> 0%
where the time goes in v2:
time: 71.1 us; the launch traced here: 70.8 us
  Pallas kernels  58.6 us (82%)
  local copies, waits for them, and re-layouts  7.63 us (11%)
  other arithmetic  3.22 us (5%)
  between operations  1.39 us (2%)
    pallas_call x1, Pallas kernels, project_blocks(): pl.pallas_call(functools.partial(spectra_kernel, dims), grid=(local_cols...  34.1 us
    pallas_call x1, Pallas kernels, exchange_modes(): pl.pallas_call(functools.partial(modes_kernel, (blk_total, map_total, 1.0...  13.6 us
    pallas_call x1, Pallas kernels, total_cross(): pl.pallas_call(functools.partial(total_kernel, blk_total, maps), out_shap...  10.8 us
    unnamed x4, local copies, waits for them, and re-layouts  1.89 us

profile of v2, /device:TPU:0, one launch (start us, length us, event | category | flops | bytes accessed | tf_op | source)
XLA Modules:
  0.0 70.8 jit_solution(12303665187152527471)
XLA Ops:
  0.6 0.0 copy-start
  0.7 1.3 %dynamic_slice.3 = s32[1]{0:T(128)} dynamic-slice(s32[32]{0:T(128)} %param.8, s32[]{:T(128)S(6)} %select_n.45), dynamic_slice_sizes={1} | dynamic-slice | bytes 12 | tf_op jit(solution)/shard_map/dynamic_slice | solution.py:472
  2.7 0.7 subtract_multiply_fusion
  3.4 0.7 broadcast_in_dim_tile.7.m_ref
  4.0 0.7 %fusion.9 = (f32[4,128]{1,0:T(4,128)S(1)}, f32[4,128]{1,0:T(4,128)S(1)}) fusion(s32[4,128]{1,0:T(4,128)} %constant.120.clone, s32[]{:T(128)} %bitcast.1), kind=kLoop, calls=%fused_computation.27 | loop fusion | flops 7168 | bytes 6148 | tf_op jit(solution)/shard_map/cos | solution.py:367
  4.7 0.6 pad_maximum_fusion.phase_ref
  5.4 0.1 divide_sqrt_fusion
  5.4 0.7 broadcast_in_dim_tile.6.z_ref
  6.1 0.7 broadcast_in_dim.4.base_ref
  6.8 1.1 %slice_divide_fusion = (f32[1,64,16,32]{1,3,2,0:T(8,128)S(1)}, f32[1,64,16,32]{1,3,2,0:T(8,128)S(1)}) fusion(f32[2,64,16,32]{1,3,2,0:T(8,128)} %param.9, f32[64,16]{0,1:T(8,128)S(1)} %divide_sqrt_fusion), kind=kLoop, calls=%fused_computation.1 | loop fusion | flops 32768 | bytes 528384 | tf_op jit(solution)/shard_map/div | solution.py:261
  7.9 0.4 copy.11
  8.3 1.2 %reshape.170.starts_ref = f32[2,16,2048]{2,1,0:T(8,128)} reshape(f32[2,16,64,32]{3,2,1,0:T(8,128)S(1)} %copy.11) | data formatting | bytes 524288 | tf_op jit(solution)/shard_map/reshape | solution.py:262
  9.4 0.0 copy-done
  9.4 0.2 copy.13
  9.7 0.9 %slice.8.sky_ref = bf16[10,128,256]{2,1,0:T(8,128)(2,1)} slice(bf16[16,128,256]{2,1,0:T(8,128)(2,1)S(1)} %bitcast.11), slice={[0:10], [0:128], [0:256]} | slice | bytes 1310720 | tf_op jit(solution)/shard_map/reshape | solution.py:382
  10.6 13.6 %shard_map.86.modes_ref = bf16[16,32,128]{2,1,0:T(8,128)(2,1)} custom-call(bf16[10,128,256]{2,1,0:T(8,128)(2,1)} %slice.8.sky_ref, bf16[128,256]{1,0:T(8,128)(2,1)} %constant.117.clone.first_ref, bf16[4,256,128]{2,1,0:T(8,128)(2,1)} %constant.118.clone.wr_ref, bf16[4,256,128]{2,1,0:T(8,128)(2,1)} %constant.119.clone.wi_ref, f32[8,128]{1,0:T(8,128)} %pad_maximum_fusion.phase_ref), custom_call_target="tpu_custom_call" | custom-call | tf_op jit(solution)/shard_map/pallas_call | solution.py:369
  24.2 34.1 %shard_map.87 = (bf16[20,64,2048]{2,1,0:T(8,128)(2,1)}, bf16[8,64,256]{2,1,0:T(8,128)(2,1)}) custom-call(f32[2,16,2048]{2,1,0:T(8,128)} %reshape.170.starts_ref, f32[1,512]{1,0:T(1,128)} %broadcast_in_dim_tile.6.z_ref, f32[1,256]{1,0:T(1,128)} %broadcast_in_dim_tile.7.m_ref, f32[16,256]{1,0:T(8,128)} %broadcast_in_dim.4.base_ref, ...), custom_call_target="tpu_custom_call" | custom-call | tf_op jit(solution)/shard_map/pallas_call | solution.py:272
  58.3 10.8 %shard_map.88 = f32[10,10,256]{2,1,0:T(8,128)} custom-call(bf16[8,64,256]{2,1,0:T(8,128)(2,1)} %get-tuple-element.5.part_ref), custom_call_target="tpu_custom_call" | custom-call | tf_op jit(solution)/shard_map/pallas_call | solution.py:440
  69.2 1.7 %copy.12 = f32[1,10,10,256]{3,0,2,1:T(1,128)} copy(f32[1,10,10,256]{3,2,1,0:T(8,128)} %bitcast.13) | data formatting | bytes 204800
  (6 shorter events, 0.1 us)
Async XLA Ops:
  0.6 8.8 %copy-start = (bf16[1,10,32768]{2,1,0:T(8,128)(2,1)S(1)}, bf16[1,10,32768]{2,1,0:T(8,128)(2,1)}, u32[]{:S(2)}) copy-start(bf16[1,10,32768]{2,1,0:T(8,128)(2,1)} %param.7) | copy-start | bytes 1966084

commit v3 on v2

--- a/solution.py
+++ b/solution.py
@@ -99,14 +99,14 @@
     return jnp.stack(stacked_rows, axis=1)
 
 
-STEP_LANES = 512
+STEP_LANES = 1024
 KDIM = 256
 GAP = 8
 
 
 def spectra_kernel(
-    dims, starts_ref, z_ref, m_ref, base_ref, modes_ref, harm_ref, cross_ref,
-    p_ref, turned_ref, pieces_ref, kap_ref, leg_ref, acc_ref,
+    dims, starts_ref, z_ref, turned_ref, pieces_ref, modes_ref, harm_ref, cross_ref,
+    leg_ref, acc_ref,
 ):
     blocks, cycles, maps, q_group, scale = dims
     step = pl.program_id(0)
@@ -116,41 +116,7 @@
 
     @pl.when(step == 0)
     def _():
-        m_row = m_ref[...]
-        piece = lax.broadcasted_iota(jnp.int32, (blocks, 256), 1) // 64
-
-        def setup(j, carry):
-            p_prev, q_prev = carry
-            degree = base_ref[...] + j.astype(jnp.float32)
-            num = 4.0 * degree * degree - 1.0
-            den = (degree - m_row) * (degree + m_row)
-            root = lax.rsqrt(num * den)
-            kappa = p_prev * p_prev
-            high = kappa.astype(jnp.bfloat16).astype(jnp.float32)
-            rest = kappa - high
-            mid = rest.astype(jnp.bfloat16).astype(jnp.float32)
-            low = rest - mid
-            pieces = jnp.where(piece == 0, high, jnp.where(piece == 1, mid, low))
-            pieces_ref[pl.ds(pl.multiple_of(j * blocks, blocks), blocks), :] = pieces.astype(
-                jnp.bfloat16
-            )
-            p_now = num * root * q_prev
-            q_now = den * root * p_prev
-            for half in range(blocks // 8):
-                p_ref[pl.ds(half * 8 * (LBLK + GAP) + j, 8, stride=LBLK + GAP), :] = p_now[
-                    half * 8 : half * 8 + 8, :128
-                ]
-            return p_now, q_now
-
-        one = jnp.ones((blocks, 256), jnp.float32)
-        lax.fori_loop(0, LBLK, setup, (one, one), unroll=4)
         acc_ref[...] = jnp.zeros_like(acc_ref)
-
-        def turn(t, _):
-            turned_ref[t] = p_ref[pl.ds(pl.multiple_of(t * (LBLK + GAP), 8), LBLK), :].T
-            return 0
-
-        lax.fori_loop(0, blocks, turn, 0)
 
     q_row = lax.broadcasted_iota(jnp.int32, (256, STEP_LANES), 0)
     q_lane = lax.broadcasted_iota(jnp.int32, (256, STEP_LANES), 1) // cycles + step * (
@@ -158,27 +124,22 @@
     )
     spread = jnp.where((q_row % 64 == q_lane) & (q_row < 192), 1.0, 0.0).astype(jnp.bfloat16)
 
-    def widen(i, _):
-        rows = pl.ds(pl.multiple_of(i * 256, 256), 256)
-        kap_ref[rows, :] = jnp.dot(
-            pieces_ref[rows, :], spread, preferred_element_type=jnp.float32
-        ) * z_ref[...]
-        return 0
-
-    lax.fori_loop(0, blocks * LBLK // 256, widen, 0, unroll=2)
-
-    def recur(j, carry):
+    run = 16
+
+    def recur(i, carry):
         older, newer = carry
-        kap = kap_ref[pl.ds(pl.multiple_of(j * blocks, blocks), blocks), :]
-        now = kap * newer - older
-        for half in range(blocks // 8):
-            for g in range(halves):
-                leg_ref[g, pl.ds(half * 8 * (LBLK + GAP) + j, 8, stride=LBLK + GAP), :] = now[
-                    half * 8 : half * 8 + 8, g * 128 : g * 128 + 128
-                ]
-        return newer, now
-
-    lax.fori_loop(0, LBLK, recur, (starts_ref[0], starts_ref[1]), unroll=8)
+        rows = pl.ds(pl.multiple_of(i * run * blocks, run * blocks), run * blocks)
+        kap = jnp.dot(pieces_ref[rows, :], spread, preferred_element_type=jnp.float32)
+        for j in range(run):
+            now = (kap[j * blocks : (j + 1) * blocks] * z_ref[...]) * newer - older
+            for half in range(blocks // 8):
+                at = pl.ds(half * 8 * (LBLK + GAP) + i * run + j, 8, stride=LBLK + GAP)
+                for g in range(halves):
+                    leg_ref[g, at, :] = now[half * 8 : half * 8 + 8, g * 128 : g * 128 + 128]
+            older, newer = newer, now
+        return older, newer
+
+    lax.fori_loop(0, LBLK // run, recur, (starts_ref[0], starts_ref[1]))
 
     rows_all = parts * q_group
     row = lax.broadcasted_iota(jnp.int32, (rows_all, 128), 0)
@@ -204,20 +165,31 @@
         wide = jnp.dot(narrow.astype(jnp.bfloat16), tile, preferred_element_type=jnp.float32)
         weights.append(jnp.where(same_q, wide, 0.0).astype(jnp.bfloat16))
 
-    def project(t, _):
-        cols = pl.ds(pl.multiple_of(t * LBLK, LBLK), LBLK)
-        src = pl.ds(pl.multiple_of(t * (LBLK + GAP), 8), LBLK)
+    def project(u, _):
+        cols = pl.ds(pl.multiple_of(u * 2 * LBLK, 2 * LBLK), 2 * LBLK)
+        sources = [
+            pl.ds(pl.multiple_of((2 * u + x) * (LBLK + GAP), 8), LBLK) for x in range(2)
+        ]
         spectra_rows = []
         for g in range(groups):
             first = pl.multiple_of((step * groups + g) * q_group, 8)
-            p_rows = turned_ref[t, pl.ds(first, q_group), :] * scale
+            p_rows = jnp.concatenate(
+                [turned_ref[2 * u + x, pl.ds(first, q_group), :] for x in range(2)], axis=1
+            ) * scale
             leg = jnp.concatenate(
-                [leg_ref[g * (KDIM // 128) + h, src, :] for h in range(KDIM // 128)], axis=1
+                [
+                    jnp.concatenate(
+                        [leg_ref[g * (KDIM // 128) + h, src, :] for h in range(KDIM // 128)],
+                        axis=1,
+                    )
+                    for src in sources
+                ],
+                axis=0,
             ).astype(jnp.bfloat16)
             out = lax.dot_general(
                 weights[g], leg, (((1,), (1,)), ((), ())), preferred_element_type=jnp.float32
             )
-            crossed = out.reshape(parts, q_group, LBLK) * p_rows[None]
+            crossed = out.reshape(parts, q_group, 2 * LBLK) * p_rows[None]
             crossed = crossed.astype(jnp.bfloat16)
             harm_ref[:, g * q_group : (g + 1) * q_group, cols] = crossed
             spectra_rows.append(crossed.astype(jnp.float32))
@@ -231,7 +203,7 @@
                 pair += 1
         return 0
 
-    lax.fori_loop(0, blocks, project, 0)
+    lax.fori_loop(0, blocks // 2, project, 0)
 
     @pl.when(step == pl.num_programs(0) - 1)
     def _():
@@ -248,7 +220,10 @@
         lax.fori_loop(0, cross_ref.shape[0], finish, 0)
 
 
-def project_blocks(legendre_starts, heights, m_float, first_l, modes, maps_count, cycle_scale, blk_total):
+def project_blocks(
+    legendre_starts, m_float, first_l, prepared, maps_count, cycle_scale, blk_total
+):
+    modes, pieces, turned, z_row = prepared
     local_cols, block_count, cycles = legendre_starts.shape[1:]
     local_len = block_count * LBLK
     q_group = KDIM // cycles
@@ -260,9 +235,6 @@
     coef = jnp.sqrt((4.0 * degree * degree - 1.0) / ((degree - m_col) * (degree + m_col)))
     starts = jnp.stack([legendre_starts[0] / coef[:, :, None], legendre_starts[1]])
     starts = jnp.transpose(starts, (0, 2, 1, 3)).reshape(2, block_count, local_cols * cycles)
-    z_row = jnp.tile(heights, STEP_LANES // cycles)[None]
-    m_row = jnp.tile(m_float, 256 // local_cols)[None]
-    base = jnp.broadcast_to(base_l[:, None], (block_count, 256))
     groups = STEP_LANES // KDIM
     step_cols = groups * q_group
     dims = (block_count, cycles, maps_count, q_group, cycle_scale)
@@ -279,8 +251,8 @@
         in_specs=[
             pl.BlockSpec((2, block_count, STEP_LANES), lambda i: (0, 0, i)),
             whole((1, STEP_LANES)),
-            whole((1, 256)),
-            whole((block_count, 256)),
+            whole(turned.shape),
+            whole(pieces.shape),
             pl.BlockSpec((step_cols // MGRP, cycles, 128), lambda i: (i, 0, 0)),
         ],
         out_specs=(
@@ -288,19 +260,18 @@
             whole((blk_total, pair_rows, share)),
         ),
         scratch_shapes=[
-            pltpu.VMEM((block_count * (LBLK + GAP), 128), jnp.float32),
-            pltpu.VMEM((block_count, 128, LBLK), jnp.float32),
-            pltpu.VMEM((local_len, 256), jnp.bfloat16),
-            pltpu.VMEM((local_len, STEP_LANES), jnp.float32),
             pltpu.VMEM((STEP_LANES // 128, block_count * (LBLK + GAP), 128), jnp.float32),
             pltpu.VMEM((pairs, 8, local_len), jnp.float32),
         ],
         compiler_params=pltpu.CompilerParams(vmem_limit_bytes=60 * 1024 * 1024),
-    )(starts, z_row, m_row, base, modes)
-
-
-def modes_kernel(totals, sky_ref, first_ref, wr_ref, wi_ref, phase_ref, out_ref,
-                 rows_ref, turned_ref, held_ref, send_sem, recv_sem):
+    )(starts, z_row, turned, pieces, modes)
+
+
+def modes_kernel(
+    totals, number_ref, sky_ref, first_ref, wr_ref, wi_ref, phase_ref,
+    out_ref, pieces_ref, scales_ref, z_ref, rows_ref, turned_ref, held_ref, p_ref,
+    send_sem, recv_sem,
+):
     blk_total, map_total, factor = totals
     maps = sky_ref.shape[0]
     count = blk_total * map_total
@@ -317,6 +288,10 @@
         )
     rows_ref[...] = jnp.zeros_like(rows_ref)
     first = first_ref[...]
+    parity = (number_ref[me] - NSIDE + 1) % 2
+    odd = jnp.full((MGRP, RES), parity, jnp.int32) == 1
+    cosines = jnp.where(odd, phase_ref[:MGRP], 1.0)
+    sines = jnp.where(odd, phase_ref[MGRP:], 0.0)
     for n in range(maps):
         section = lax.dot_general(
             sky_ref[n], first, (((0,), (0,)), ((), ())), preferred_element_type=jnp.float32
@@ -328,7 +303,7 @@
             wave_im = wi_ref[c].astype(jnp.float32)
             real = jnp.sum(wave_re * part_re - wave_im * part_im, axis=0, keepdims=True)
             imag = jnp.sum(wave_re * part_im + wave_im * part_re, axis=0, keepdims=True)
-            cos, sin = phase_ref[c : c + 1], phase_ref[MGRP + c : MGRP + c + 1]
+            cos, sin = cosines[c : c + 1], sines[c : c + 1]
             row = c * 2 * maps + n
             rows_ref[row : row + 1, :] = factor * (cos * real + sin * imag)
             rows_ref[row + maps : row + maps + 1, :] = factor * (cos * imag - sin * real)
@@ -349,6 +324,7 @@
     for i in range(1, count):
         copy_to(lax.rem(me + i, count), me).start()
     held_ref[me] = turned_ref[pl.ds(pl.multiple_of(me_blk * share, share), share), :]
+    prepare(blk_total, number_ref, pieces_ref, scales_ref, z_ref, p_ref)
     for i in range(1, count):
         peer = lax.rem(me + i, count)
         copy_to(peer, peer).wait_recv()
@@ -358,28 +334,83 @@
     out_ref[...] = jnp.swapaxes(gathered, 0, 1).astype(jnp.bfloat16)
 
 
-def exchange_modes(sky_maps, parity, blk_total, map_total):
+def prepare(blk_total, number_ref, pieces_ref, scales_ref, z_ref, p_ref):
+    blocks = scales_ref.shape[0]
+    local_cols = MGRP * RES // blk_total
+    lane = lax.broadcasted_iota(jnp.int32, z_ref.shape, 1) % number_ref.shape[0]
+    numbers = jnp.zeros(z_ref.shape, jnp.int32)
+    for r in range(number_ref.shape[0]):
+        numbers = jnp.where(lane == r, number_ref[r], numbers)
+    z_ref[...] = cycle_height(numbers)
+    lane = lax.broadcasted_iota(jnp.int32, (blocks, 256), 1)
+    piece = lane // local_cols
+    column = lax.axis_index("blk") * local_cols + lane % local_cols
+    m_row = (MSTART + RES * (column % MGRP) + column // MGRP).astype(jnp.float32)
+    block = lax.broadcasted_iota(jnp.int32, (blocks, 256), 0)
+    base = LSTART + (lax.axis_index("map") * blocks + block) * LBLK
+
+    def setup(j, carry):
+        p_prev, q_prev = carry
+        degree = (base + j).astype(jnp.float32)
+        num = 4.0 * degree * degree - 1.0
+        den = (degree - m_row) * (degree + m_row)
+        root = lax.rsqrt(num * den)
+        kappa = p_prev * p_prev
+        high = kappa.astype(jnp.bfloat16).astype(jnp.float32)
+        rest = kappa - high
+        mid = rest.astype(jnp.bfloat16).astype(jnp.float32)
+        low = rest - mid
+        pieces = jnp.where(piece == 0, high, jnp.where(piece == 1, mid, low))
+        pieces_ref[pl.ds(pl.multiple_of(j * blocks, blocks), blocks), :] = pieces.astype(
+            jnp.bfloat16
+        )
+        p_now = num * root * q_prev
+        q_now = den * root * p_prev
+        for half in range(blocks // 8):
+            p_ref[pl.ds(half * 8 * (LBLK + GAP) + j, 8, stride=LBLK + GAP), :] = p_now[
+                half * 8 : half * 8 + 8, :128
+            ]
+        return p_now, q_now
+
+    one = jnp.ones((blocks, 256), jnp.float32)
+    lax.fori_loop(0, LBLK, setup, (one, one), unroll=4)
+
+    def turn(t, _):
+        turned = p_ref[pl.ds(pl.multiple_of(t * (LBLK + GAP), 8), LBLK), :].T
+        scales_ref[t] = turned[:local_cols]
+        return 0
+
+    lax.fori_loop(0, blocks, turn, 0)
+
+
+def exchange_modes(sky_maps, cycle_number, block_count, blk_total, map_total):
     _, maps, cycle_len = sky_maps.shape
     first_table, wave_re, wave_im = constant_tables(cycle_len)
     m_value = MSTART + np.arange(MGRP)[:, None] * RES + np.arange(RES)[None, :]
-    m_value = jnp.asarray(m_value, jnp.int32)
-    angle = math.pi / cycle_len * (m_value * parity[0] % (2 * cycle_len)).astype(jnp.float32)
-    phase = jnp.concatenate([jnp.cos(angle), jnp.sin(angle)], axis=0)
+    angle = np.float32(math.pi / cycle_len) * (m_value % (2 * cycle_len)).astype(np.float32)
+    phase = jnp.asarray(np.concatenate([np.cos(angle), np.sin(angle)], axis=0))
     count = blk_total * map_total
     return pl.pallas_call(
         functools.partial(modes_kernel, (blk_total, map_total, 1.0 / math.sqrt(cycle_len))),
-        out_shape=jax.ShapeDtypeStruct((RES // blk_total, count, 128), jnp.bfloat16),
-        in_specs=[pl.BlockSpec(memory_space=pltpu.VMEM)] * 5,
-        out_specs=pl.BlockSpec(memory_space=pltpu.VMEM),
+        out_shape=(
+            jax.ShapeDtypeStruct((RES // blk_total, count, 128), jnp.bfloat16),
+            jax.ShapeDtypeStruct((block_count * LBLK, 256), jnp.bfloat16),
+            jax.ShapeDtypeStruct((block_count, MGRP * RES // blk_total, LBLK), jnp.float32),
+            jax.ShapeDtypeStruct((1, STEP_LANES), jnp.float32),
+        ),
+        in_specs=[pl.BlockSpec(memory_space=pltpu.SMEM)]
+        + [pl.BlockSpec(memory_space=pltpu.VMEM)] * 5,
+        out_specs=(pl.BlockSpec(memory_space=pltpu.VMEM),) * 4,
         scratch_shapes=[
             pltpu.VMEM((128, RES), jnp.float32),
             pltpu.VMEM((RES, 128), jnp.bfloat16),
             pltpu.VMEM((count, RES // blk_total, 128), jnp.bfloat16),
+            pltpu.VMEM((block_count * (LBLK + GAP), 128), jnp.float32),
             pltpu.SemaphoreType.DMA((count,)),
             pltpu.SemaphoreType.DMA((count,)),
         ],
         compiler_params=pltpu.CompilerParams(collective_id=0, has_side_effects=True),
-    )(sky_maps.reshape(maps, RES, cycle_len // RES), first_table, wave_re, wave_im, phase)
+    )(cycle_number, sky_maps.reshape(maps, RES, cycle_len // RES), first_table, wave_re, wave_im, phase)
 
 
 def constant_tables(cycle_len):
@@ -427,9 +458,9 @@
     pair = 0
     for i in range(maps):
         for k in range(i, maps):
-            out_ref[i, k : k + 1, :] = total[pair : pair + 1]
+            out_ref[i, k] = total[pair : pair + 1]
             if k > i:
-                out_ref[k, i : i + 1, :] = total[pair : pair + 1]
+                out_ref[k, i] = total[pair : pair + 1]
             pair += 1
     for peer in order:
         copy_to(peer, me).wait_send()
@@ -439,7 +470,7 @@
     blk_total, pair_rows, share = cross.shape
     return pl.pallas_call(
         functools.partial(total_kernel, blk_total, maps),
-        out_shape=jax.ShapeDtypeStruct((maps, maps, share), jnp.float32),
+        out_shape=jax.ShapeDtypeStruct((maps, maps, 1, share), jnp.float32),
         in_specs=[pl.BlockSpec(memory_space=pltpu.VMEM)],
         out_specs=pl.BlockSpec(memory_space=pltpu.VMEM),
         scratch_shapes=[
@@ -468,20 +499,17 @@
     _, maps_count, _ = sky_maps.shape
     map_total = lax.axis_size("map")
     blk_total = lax.axis_size("blk")
-    row = lax.axis_index("blk") * map_total + lax.axis_index("map")
-    parity = (lax.dynamic_slice_in_dim(cycle_number, row, 1) - NSIDE + 1) % 2
-    modes = exchange_modes(sky_maps, parity, blk_total, map_total)
-    heights = cycle_height(cycle_number)
     local_cols, block_count, cycles = legendre_starts.shape[1:]
+    prepared = exchange_modes(sky_maps, cycle_number, block_count, blk_total, map_total)
     column = lax.axis_index("blk") * local_cols + jnp.arange(local_cols, dtype=jnp.int32)
     m_float = (MSTART + RES * (column % MGRP) + column // MGRP).astype(jnp.float32)
     first_l = LSTART + lax.axis_index("map") * block_count * LBLK
     cycle_scale = 1.0 / math.sqrt(cycles)
     harmonics, cross = project_blocks(
-        legendre_starts, heights, m_float, first_l, modes, maps_count, cycle_scale, blk_total
+        legendre_starts, m_float, first_l, prepared, maps_count, cycle_scale, blk_total
     )
     spectra = total_cross(cross, maps_count)
-    return (jnp.transpose(harmonics, (1, 0, 2)), spectra[None])
+    return (jnp.transpose(harmonics, (1, 0, 2)), jnp.transpose(spectra, (2, 0, 1, 3)))
 
 
 def body(sky_maps, cycle_number, legendre_starts):

time: 71.1 us -> 53.3 us (0.75)
  Pallas kernels: 58.6 us -> 46.9 us
  local copies, waits for them, and re-layouts: 7.63 us -> 4.21 us
  other arithmetic: 3.22 us -> 1.3 us
    pallas_call x1, Pallas kernels: 34.1 us -> 21.6 us  [project_blocks(): pl.pallas_call(functools.partial(spectra_kernel, dims), grid=(local_cols...]
    dynamic_slice x1 -> x0, local copies, waits for them, and re-layouts: 1.33 us -> none  [fast_body(): parity = (lax.dynamic_slice_in_dim(cycle_number, row, 1) - NSIDE + 1) % 2]
    another operation x4 -> x0, local copies, waits for them, and re-layouts: 1.32 us -> none  [the longest x2 0.66 us: project_blocks(): z_row = jnp.tile(heights, STEP_LANES // cycles)[None]]
    pallas_call x1, Pallas kernels: 13.6 us -> 14.4 us  [exchange_modes(): pl.pallas_call(functools.partial(modes_kernel, (blk_total, map_total, 1.0...]
    cos x1 -> x0, other arithmetic: 0.73 us -> none  [exchange_modes(): phase = jnp.concatenate([jnp.cos(angle), jnp.sin(angle)], axis=0)]
where the time goes in v3:
time: 53.3 us; the launch traced here: 53.1 us
  Pallas kernels  46.9 us (88%)
  local copies, waits for them, and re-layouts  4.21 us (8%)
  other arithmetic  1.3 us (2%)
  between operations  0.7 us (1%)
    pallas_call x1, Pallas kernels, project_blocks(): pl.pallas_call(functools.partial(spectra_kernel, dims), grid=(local_cols...  21.6 us
    pallas_call x1, Pallas kernels, exchange_modes(): pl.pallas_call(functools.partial(modes_kernel, (blk_total, map_total, 1.0...  14.4 us
    pallas_call x1, Pallas kernels, total_cross(): pl.pallas_call(functools.partial(total_kernel, blk_total, maps), out_shap...  10.8 us
    unnamed x4, local copies, waits for them, and re-layouts  1.77 us
    reshape x1, local copies, waits for them, and re-layouts, project_blocks(): jnp.transpose(starts, (0, 2, 1, 3))  1.2 us
    div x1, other arithmetic, project_blocks(): legendre_starts[0] / coef[:, :, None]  1.15 us

profile of v3, /device:TPU:0, one launch (start us, length us, event | category | flops | bytes accessed | tf_op | source)
XLA Modules:
  0.0 53.1 jit_solution(4103564434602106696)
XLA Ops:
  0.6 0.0 copy-start
  0.7 0.1 divide_sqrt_fusion
  0.8 1.1 %slice_divide_fusion = (f32[1,64,16,32]{1,3,2,0:T(8,128)S(1)}, f32[1,64,16,32]{1,3,2,0:T(8,128)S(1)}) fusion(f32[2,64,16,32]{1,3,2,0:T(8,128)} %param.9, f32[64,16]{0,1:T(8,128)S(1)} %divide_sqrt_fusion), kind=kLoop, calls=%fused_computation.1 | loop fusion | flops 32768 | bytes 528384 | tf_op jit(solution)/shard_map/div | solution.py:236
  2.0 0.4 copy.10
  2.3 1.2 %reshape.128.starts_ref = f32[2,16,2048]{2,1,0:T(8,128)} reshape(f32[2,16,64,32]{3,2,1,0:T(8,128)S(1)} %copy.10) | data formatting | bytes 524288 | tf_op jit(solution)/shard_map/reshape | solution.py:237
  3.5 0.0 copy-done
  3.5 0.2 copy.11
  3.8 0.9 %slice.8.sky_ref = bf16[10,128,256]{2,1,0:T(8,128)(2,1)} slice(bf16[16,128,256]{2,1,0:T(8,128)(2,1)S(1)} %bitcast.10), slice={[0:10], [0:128], [0:256]} | slice | bytes 1310720 | tf_op jit(solution)/shard_map/reshape | solution.py:413
  4.6 14.4 %shard_map.86 = (bf16[16,32,128]{2,1,0:T(8,128)(2,1)}, bf16[2048,256]{1,0:T(8,128)(2,1)}, f32[16,64,128]{2,1,0:T(8,128)}, f32[1,1024]{1,0:T(1,128)}) custom-call(s32[32]{0:T(128)} %number_ref.1, bf16[10,128,256]{2,1,0:T(8,128)(2,1)} %slice.8.sky_ref, bf16[128,256]{1,0:T(8,128)(2,1)} %constant.65.clone.first_ref, bf16[4,256,128]{2,1,0:T(8,128)(2,1)} %constant.66.clone.wr_ref, ...), custom_call_target="tpu_custom_call" | custom-call | tf_op jit(solution)/shard_map/pallas_call | solution.py:393
  19.1 21.6 %shard_map.87 = (bf16[20,64,2048]{2,1,0:T(8,128)(2,1)}, bf16[8,64,256]{2,1,0:T(8,128)(2,1)}) custom-call(f32[2,16,2048]{2,1,0:T(8,128)} %reshape.128.starts_ref, f32[1,1024]{1,0:T(1,128)} %get-tuple-element.8.z_ref, f32[16,64,128]{2,1,0:T(8,128)} %get-tuple-element.9.turned_ref, bf16[2048,256]{1,0:T(8,128)(2,1)} %get-tuple-element.10.pieces_ref, ...), custom_call_target="tpu_custom_call" | custom-call | tf_op jit(solution)/shard_map/pallas_call | solution.py:244
  40.7 10.8 %shard_map.88 = f32[10,10,1,256]{3,2,1,0:T(1,128)} custom-call(bf16[8,64,256]{2,1,0:T(8,128)(2,1)} %get-tuple-element.13.part_ref), custom_call_target="tpu_custom_call" | custom-call | tf_op jit(solution)/shard_map/pallas_call | solution.py:471
  51.5 1.5 %copy.13 = f32[1,10,10,256]{3,0,2,1:T(1,128)} copy(f32[1,10,10,256]{3,0,2,1:T(1,128)} %bitcast.12) | data formatting | bytes 204800
  (3 shorter events, 0.1 us)
Async XLA Ops:
  0.6 2.9 %copy-start = (bf16[1,10,32768]{2,1,0:T(8,128)(2,1)S(1)}, bf16[1,10,32768]{2,1,0:T(8,128)(2,1)}, u32[]{:S(2)}) copy-start(bf16[1,10,32768]{2,1,0:T(8,128)(2,1)} %param.7) | copy-start | bytes 1966084

commit v4 on v3

--- a/solution.py
+++ b/solution.py
@@ -238,7 +238,7 @@
     groups = STEP_LANES // KDIM
     step_cols = groups * q_group
     dims = (block_count, cycles, maps_count, q_group, cycle_scale)
-    pair_rows = -(-pairs // 16) * 16
+    pair_rows = -(-pairs // 8) * 8
     share = local_len // blk_total
     whole = lambda shape: pl.BlockSpec(shape, lambda i: (0,) * len(shape))
     return pl.pallas_call(

time: 53.3 us -> 52.9 us (level)
  no operation moved by 1% of the time
where the time goes in v4:
time: 52.9 us; the launch traced here: 52.6 us
  Pallas kernels  46.4 us (88%)
  local copies, waits for them, and re-layouts  4.2 us (8%)
  other arithmetic  1.3 us (2%)
  between operations  0.7 us (1%)
    pallas_call x1, Pallas kernels, project_blocks(): pl.pallas_call(functools.partial(spectra_kernel, dims), grid=(local_cols...  21.6 us
    pallas_call x1, Pallas kernels, exchange_modes(): pl.pallas_call(functools.partial(modes_kernel, (blk_total, map_total, 1.0...  14.5 us
    pallas_call x1, Pallas kernels, total_cross(): pl.pallas_call(functools.partial(total_kernel, blk_total, maps), out_shap...  10.3 us
    unnamed x4, local copies, waits for them, and re-layouts  1.77 us
    reshape x1, local copies, waits for them, and re-layouts, project_blocks(): jnp.transpose(starts, (0, 2, 1, 3))  1.19 us
    div x1, other arithmetic, project_blocks(): legendre_starts[0] / coef[:, :, None]  1.15 us

profile of v4, /device:TPU:0, one launch (start us, length us, event | category | flops | bytes accessed | tf_op | source)
XLA Modules:
  0.0 52.6 jit_solution(17211845453036951225)
XLA Ops:
  0.6 0.0 copy-start
  0.7 0.1 divide_sqrt_fusion
  0.8 1.1 %slice_divide_fusion = (f32[1,64,16,32]{1,3,2,0:T(8,128)S(1)}, f32[1,64,16,32]{1,3,2,0:T(8,128)S(1)}) fusion(f32[2,64,16,32]{1,3,2,0:T(8,128)} %param.9, f32[64,16]{0,1:T(8,128)S(1)} %divide_sqrt_fusion), kind=kLoop, calls=%fused_computation.1 | loop fusion | flops 32768 | bytes 528384 | tf_op jit(solution)/shard_map/div | solution.py:236
  2.0 0.4 copy.10
  2.3 1.2 %reshape.128.starts_ref = f32[2,16,2048]{2,1,0:T(8,128)} reshape(f32[2,16,64,32]{3,2,1,0:T(8,128)S(1)} %copy.10) | data formatting | bytes 524288 | tf_op jit(solution)/shard_map/reshape | solution.py:237
  3.5 0.0 copy-done
  3.5 0.2 copy.11
  3.8 0.9 %slice.8.sky_ref = bf16[10,128,256]{2,1,0:T(8,128)(2,1)} slice(bf16[16,128,256]{2,1,0:T(8,128)(2,1)S(1)} %bitcast.10), slice={[0:10], [0:128], [0:256]} | slice | bytes 1310720 | tf_op jit(solution)/shard_map/reshape | solution.py:413
  4.6 14.5 %shard_map.86 = (bf16[16,32,128]{2,1,0:T(8,128)(2,1)}, bf16[2048,256]{1,0:T(8,128)(2,1)}, f32[16,64,128]{2,1,0:T(8,128)}, f32[1,1024]{1,0:T(1,128)}) custom-call(s32[32]{0:T(128)} %number_ref.1, bf16[10,128,256]{2,1,0:T(8,128)(2,1)} %slice.8.sky_ref, bf16[128,256]{1,0:T(8,128)(2,1)} %constant.65.clone.first_ref, bf16[4,256,128]{2,1,0:T(8,128)(2,1)} %constant.66.clone.wr_ref, ...), custom_call_target="tpu_custom_call" | custom-call | tf_op jit(solution)/shard_map/pallas_call | solution.py:393
  19.1 21.6 %shard_map.87 = (bf16[20,64,2048]{2,1,0:T(8,128)(2,1)}, bf16[8,56,256]{2,1,0:T(8,128)(2,1)}) custom-call(f32[2,16,2048]{2,1,0:T(8,128)} %reshape.128.starts_ref, f32[1,1024]{1,0:T(1,128)} %get-tuple-element.8.z_ref, f32[16,64,128]{2,1,0:T(8,128)} %get-tuple-element.9.turned_ref, bf16[2048,256]{1,0:T(8,128)(2,1)} %get-tuple-element.10.pieces_ref, ...), custom_call_target="tpu_custom_call" | custom-call | tf_op jit(solution)/shard_map/pallas_call | solution.py:244
  40.7 10.3 %shard_map.88 = f32[10,10,1,256]{3,2,1,0:T(1,128)} custom-call(bf16[8,56,256]{2,1,0:T(8,128)(2,1)} %get-tuple-element.13.part_ref), custom_call_target="tpu_custom_call" | custom-call | tf_op jit(solution)/shard_map/pallas_call | solution.py:471
  51.1 1.5 %copy.13 = f32[1,10,10,256]{3,0,2,1:T(1,128)} copy(f32[1,10,10,256]{3,0,2,1:T(1,128)} %bitcast.12) | data formatting | bytes 204800
  (3 shorter events, 0.1 us)
Async XLA Ops:
  0.6 2.9 %copy-start = (bf16[1,10,32768]{2,1,0:T(8,128)(2,1)S(1)}, bf16[1,10,32768]{2,1,0:T(8,128)(2,1)}, u32[]{:S(2)}) copy-start(bf16[1,10,32768]{2,1,0:T(8,128)(2,1)} %param.7) | copy-start | bytes 1966084
